TPU v7x, 32 devices: a whole 2x2x4 slice. The times are simulated.
32 devices in a mesh: dp: 8 (over y, x, core), seg: 4 (over z).
Axes of the slice: x: 2, y: 2, z: 4, core: 2. Of those that a mesh axis runs over, the one named last changes fastest.
Arguments:
- tokens: bfloat16 [2, 16, 2048, 768], P(None, 'dp', 'seg'), may hold values from -6 to 6
- cotangent: bfloat16 [2, 16, 2048, 768], P(None, 'dp', 'seg'), may hold values from -6 to 6
- document_ids: int32 [2, 16, 16], P(None, 'dp'), may hold values from 0 to 3, never falling along the last dimension, each value on 1 to 8 neighbouring positions
- position_ids: int32 [2, 16, 16], P(None, 'dp'), may hold values from 0 to 63
- project_in: bfloat16 [2, 768, 2304], P(None, 'dp', 'seg'), may hold values from -0.3125 to 0.3125
- project_out: bfloat16 [2, 768, 768], P(None, 'dp', 'seg'), may hold values from -0.875 to 0.875
- up_weight: bfloat16 [2, 768, 3072], P(None, 'dp', 'seg'), may hold values from -0.21875 to 0.21875
- down_weight: bfloat16 [2, 3072, 768], P(None, 'dp', 'seg'), may hold values from -0.109375 to 0.109375
- norm_gains: bfloat16 [2, 768, 2], P(None, 'dp'), may hold values from 0.5 to 1.5
- biases: bfloat16 [2, 768, 6], P(None, 'dp'), may hold values from -1.25 to 1.25
- up_bias: bfloat16 [2, 3072], P(None, 'dp'), may hold values from -1.25 to 1.25
- position_table: bfloat16 [768, 64], P('dp'), may hold values from -3 to 3
Outputs:
- layer_out: bfloat16 [2, 16, 2048, 768], P(None, 'dp', 'seg')
- input_grad: float32 [2, 16, 2048, 768], P(None, 'dp', 'seg')
- project_in_grad: float32 [2, 768, 2304], P(None, 'dp', 'seg')
- project_out_grad: float32 [2, 768, 768], P(None, 'dp', 'seg')
- up_weight_grad: float32 [2, 768, 3072], P(None, 'dp', 'seg')
- down_weight_grad: float32 [2, 3072, 768], P(None, 'dp', 'seg')
- norm_gains_grad: float32 [2, 768, 2], P(None, 'dp')
- biases_grad: float32 [2, 768, 6], P(None, 'dp')
- up_bias_grad: float32 [2, 3072], P(None, 'dp')
- position_table_grad: float32 [768, 64], P('dp')
Inputs may be any that keep to these rules, and one draw needn't show every extreme that they name: `document_ids`: document ids count from 0 in every row and never fall along it; a document has 1 to 8 segments.
All inputs are finite; a program needn't handle non-finite values.
Results may differ from a plain program's by a relative error of at most 0.028.
Values may be sent and summed in bfloat16 or wider, within the bound.
A program may use at most 320 MiB of HBM per device.

v0:
```python
import jax
import jax.numpy as jnp
from jax import lax
from jax.sharding import PartitionSpec as P

HEADS = 12
HD = 64
SEGLEN = 128
POS = 64


NORM_EPS = 1e-05
PRECISE = lax.Precision.HIGHEST


def norm_apply(inputs, norm_gain, norm_shift):
    average = jnp.mean(inputs, axis=-1, keepdims=True)
    centered = inputs - average
    variance = jnp.mean(centered * centered, axis=-1, keepdims=True)
    return centered * lax.rsqrt(variance + NORM_EPS) * norm_gain + norm_shift


def norm_backward(inputs, norm_gain, norm_shift, upstream):
    unused_out, pull_back = jax.vjp(norm_apply, inputs, norm_gain, norm_shift)
    return pull_back(upstream)


def gelu_exact(inputs):
    return jax.nn.gelu(inputs, approximate=False)


def soft_scores(queries, key_rows, same_document):
    scores = jnp.einsum(
        "gqhe,gkhe->ghqk", queries, key_rows, preferred_element_type=jnp.float32
    ) * HD ** (-0.5)
    if same_document is not None:
        scores = jnp.where(same_document[:, None, :, :], scores, -1e30)
    return scores


def block_forward(source, residual, weights, same_document):
    project_in, project_out, up_weight, down_weight, norm_gains, biases, up_bias = weights
    features = source.shape[-1]
    leading = source.shape[:-1]
    head_shape = leading + (HEADS, HD)
    joined = jnp.einsum("gld,de->gle", source, project_in, preferred_element_type=jnp.float32)
    queries = (joined[..., :features] + biases[:, 0]).astype(jnp.bfloat16)
    key_rows = joined[..., features : 2 * features].astype(jnp.bfloat16)
    values = (joined[..., 2 * features :] + biases[:, 1]).astype(jnp.bfloat16)
    scores = soft_scores(queries.reshape(head_shape), key_rows.reshape(head_shape), same_document)
    log_total = jax.nn.logsumexp(scores, axis=-1, keepdims=True)
    attention = jnp.exp(scores - log_total).astype(jnp.bfloat16)
    context = jnp.einsum(
        "ghqk,gkhe->gqhe", attention, values.reshape(head_shape), preferred_element_type=jnp.float32
    )
    context = context.reshape(leading + (features,)).astype(jnp.bfloat16)
    mixed_input = residual + (
        jnp.einsum("gld,de->gle", context, project_out, preferred_element_type=jnp.float32)
        + biases[:, 2]
    )
    first_norm = norm_apply(mixed_input, norm_gains[:, 0], biases[:, 4])
    first_low = first_norm.astype(jnp.bfloat16)
    pre_gelu = (
        jnp.einsum("gld,df->glf", first_low, up_weight, preferred_element_type=jnp.float32)
        + up_bias
    )
    activation = gelu_exact(pre_gelu).astype(jnp.bfloat16)
    second_input = first_norm + (
        jnp.einsum("glf,fd->gld", activation, down_weight, preferred_element_type=jnp.float32)
        + biases[:, 3]
    )
    result = norm_apply(second_input, norm_gains[:, 1], biases[:, 5])
    stored = (
        queries,
        key_rows,
        values,
        log_total,
        context,
        mixed_input,
        first_low,
        pre_gelu,
        activation,
        second_input,
    )
    return (result, stored)


def block_backward(source, stored, weights, same_document, upstream):
    project_in, project_out, up_weight, down_weight, norm_gains, biases, up_bias = weights
    (
        queries,
        key_rows,
        values,
        log_total,
        context,
        mixed_input,
        first_low,
        pre_gelu,
        activation,
        second_input,
    ) = stored
    features = source.shape[-1]
    leading = source.shape[:-1]
    head_shape = leading + (HEADS, HD)
    sum_axes = (0, 1)
    second_grad, gain_two, shift_two = norm_backward(
        second_input, norm_gains[:, 1], biases[:, 5], upstream
    )
    branch_grad = second_grad.astype(jnp.bfloat16)
    down_grad = jnp.einsum(
        "glf,gld->fd", activation, branch_grad, preferred_element_type=jnp.float32
    )
    activation_grad = jnp.einsum(
        "gld,fd->glf", branch_grad, down_weight, preferred_element_type=jnp.float32
    )
    unused_out, gelu_pull = jax.vjp(gelu_exact, pre_gelu)
    pre_gelu_grad = gelu_pull(activation_grad)[0].astype(jnp.bfloat16)
    up_grad = jnp.einsum(
        "gld,glf->df", first_low, pre_gelu_grad, preferred_element_type=jnp.float32
    )
    first_grad = second_grad + jnp.einsum(
        "glf,df->gld", pre_gelu_grad, up_weight, preferred_element_type=jnp.float32
    )
    mixed_grad, gain_one, shift_one = norm_backward(
        mixed_input, norm_gains[:, 0], biases[:, 4], first_grad
    )
    mixed_low = mixed_grad.astype(jnp.bfloat16)
    outward_grad = jnp.einsum("gld,gle->de", context, mixed_low, preferred_element_type=jnp.float32)
    context_grad = jnp.einsum(
        "gle,de->gld", mixed_low, project_out, preferred_element_type=jnp.float32
    )
    context_grad = context_grad.astype(jnp.bfloat16).reshape(head_shape)
    query_heads = queries.reshape(head_shape)
    key_heads = key_rows.reshape(head_shape)
    scores = soft_scores(query_heads, key_heads, same_document)
    attention = jnp.exp(scores - log_total)
    value_grad = jnp.einsum(
        "ghqk,gqhe->gkhe",
        attention.astype(jnp.bfloat16),
        context_grad,
        preferred_element_type=jnp.float32,
    )
    soft_grad = jnp.einsum(
        "gqhe,gkhe->ghqk",
        context_grad,
        values.reshape(head_shape),
        preferred_element_type=jnp.float32,
    )
    score_grad = attention * (soft_grad - jnp.sum(soft_grad * attention, axis=-1, keepdims=True))
    score_grad = score_grad.astype(jnp.bfloat16)
    query_grad = jnp.einsum(
        "ghqk,gkhe->gqhe", score_grad, key_heads, preferred_element_type=jnp.float32
    ) * HD ** (-0.5)
    key_grad = jnp.einsum(
        "ghqk,gqhe->gkhe", score_grad, query_heads, preferred_element_type=jnp.float32
    ) * HD ** (-0.5)
    joined_grad = jnp.concatenate(
        [
            query_grad.reshape(leading + (features,)),
            key_grad.reshape(leading + (features,)),
            value_grad.reshape(leading + (features,)),
        ],
        axis=-1,
    ).astype(jnp.bfloat16)
    inward_grad = jnp.einsum("gld,gle->de", source, joined_grad, preferred_element_type=jnp.float32)
    source_grad = mixed_grad + jnp.einsum(
        "gle,de->gld", joined_grad, project_in, preferred_element_type=jnp.float32
    )
    bias_grad = jnp.stack(
        [
            jnp.sum(joined_grad[..., :features], axis=sum_axes, dtype=jnp.float32),
            jnp.sum(joined_grad[..., 2 * features :], axis=sum_axes, dtype=jnp.float32),
            jnp.sum(mixed_low, axis=sum_axes, dtype=jnp.float32),
            jnp.sum(branch_grad, axis=sum_axes, dtype=jnp.float32),
            shift_one,
            shift_two,
        ],
        axis=-1,
    )
    gain_grad = jnp.stack([gain_one, gain_two], axis=-1)
    bias_up_grad = jnp.sum(pre_gelu_grad, axis=sum_axes, dtype=jnp.float32)
    return (
        source_grad,
        (inward_grad, outward_grad, up_grad, down_grad, gain_grad, bias_grad, bias_up_grad),
    )


def pick_block(weights, which_block):
    return (
        weights[0][which_block],
        weights[1][which_block],
        weights[2][which_block],
        weights[3][which_block],
        weights[4][which_block].astype(jnp.float32),
        weights[5][which_block].astype(jnp.float32),
        weights[6][which_block].astype(jnp.float32),
    )


def shards(
    tokens,
    cotangent,
    document_ids,
    position_ids,
    project_in,
    project_out,
    up_weight,
    down_weight,
    norm_gains,
    biases,
    up_bias,
    position_table,
):
    shard_index = lax.axis_index("seg")
    first_shard = (shard_index == 0).astype(jnp.float32)
    micro_count, row_count, row_tokens, features = tokens.shape
    segment_count = row_tokens // SEGLEN
    group_count = row_count * segment_count
    slot_ids = jnp.arange(POS, dtype=jnp.int32)
    outputs = []
    input_grads = []
    totals = None
    for micro_step in range(micro_count):
        weights = (
            lax.all_gather(
                lax.all_gather(project_in, "seg", axis=2, tiled=True), "dp", axis=1, tiled=True
            ),
            lax.all_gather(
                lax.all_gather(project_out, "seg", axis=2, tiled=True), "dp", axis=1, tiled=True
            ),
            lax.all_gather(
                lax.all_gather(up_weight, "seg", axis=2, tiled=True), "dp", axis=1, tiled=True
            ),
            lax.all_gather(
                lax.all_gather(down_weight, "seg", axis=2, tiled=True), "dp", axis=1, tiled=True
            ),
            lax.all_gather(norm_gains, "dp", axis=1, tiled=True),
            lax.all_gather(biases, "dp", axis=1, tiled=True),
            lax.all_gather(up_bias, "dp", axis=1, tiled=True),
            lax.all_gather(position_table, "dp", axis=0, tiled=True),
        )
        local_weights = pick_block(weights, 0)
        cross_weights = pick_block(weights, 1)
        gathered_table = weights[7]
        segments = tokens[micro_step].reshape(group_count, SEGLEN, features)
        local_out, local_stored = block_forward(
            segments, segments.astype(jnp.float32), local_weights, None
        )
        class_own = (
            local_out[:, 0, :].astype(jnp.bfloat16).reshape(row_count, segment_count, features)
        )
        class_rows = lax.all_gather(class_own, "seg", axis=1, tiled=True)
        one_hot = (position_ids[micro_step][:, :, None] == slot_ids).astype(jnp.bfloat16)
        cross_in = class_rows.astype(jnp.float32) + jnp.einsum(
            "rsp,dp->rsd", one_hot, gathered_table, preferred_element_type=jnp.float32
        )
        documents = document_ids[micro_step]
        same_document = documents[:, :, None] == documents[:, None, :]
        cross_low = cross_in.astype(jnp.bfloat16)
        cross_out, cross_stored = block_forward(cross_low, cross_in, cross_weights, same_document)
        cross_own = lax.dynamic_slice_in_dim(
            cross_out, shard_index * segment_count, segment_count, 1
        )
        merged = local_out.at[:, 0, :].set(cross_own.reshape(group_count, features))
        outputs.append(merged.astype(jnp.bfloat16).reshape(row_count, row_tokens, features))
        weights = (
            lax.all_gather(
                lax.all_gather(project_in, "seg", axis=2, tiled=True), "dp", axis=1, tiled=True
            ),
            lax.all_gather(
                lax.all_gather(project_out, "seg", axis=2, tiled=True), "dp", axis=1, tiled=True
            ),
            lax.all_gather(
                lax.all_gather(up_weight, "seg", axis=2, tiled=True), "dp", axis=1, tiled=True
            ),
            lax.all_gather(
                lax.all_gather(down_weight, "seg", axis=2, tiled=True), "dp", axis=1, tiled=True
            ),
            lax.all_gather(norm_gains, "dp", axis=1, tiled=True),
            lax.all_gather(biases, "dp", axis=1, tiled=True),
            lax.all_gather(up_bias, "dp", axis=1, tiled=True),
            lax.all_gather(position_table, "dp", axis=0, tiled=True),
        )
        local_weights = pick_block(weights, 0)
        cross_weights = pick_block(weights, 1)
        upstream = cotangent[micro_step].reshape(group_count, SEGLEN, features)
        class_grad_own = upstream[:, 0, :].reshape(row_count, segment_count, features)
        class_grads = lax.all_gather(class_grad_own, "seg", axis=1, tiled=True)
        cross_grad, cross_terms = block_backward(
            cross_low, cross_stored, cross_weights, same_document, class_grads.astype(jnp.float32)
        )
        table_grad = jnp.einsum(
            "rsd,rsp->dp", cross_grad, one_hot.astype(jnp.float32), precision=PRECISE
        )
        own_grad = lax.dynamic_slice_in_dim(
            cross_grad, shard_index * segment_count, segment_count, 1
        )
        local_upstream = (
            upstream.astype(jnp.float32).at[:, 0, :].set(own_grad.reshape(group_count, features))
        )
        token_grad, local_terms = block_backward(
            segments, local_stored, local_weights, None, local_upstream
        )
        input_grads.append(token_grad.reshape(row_count, row_tokens, features))
        gradients = tuple(
            (
                jnp.stack([local_term, cross_term * first_shard])
                for local_term, cross_term in zip(local_terms, cross_terms)
            )
        ) + (table_grad * first_shard,)
        small_sums = lax.psum(
            (
                lax.psum_scatter(
                    gradients[4].astype(jnp.bfloat16), "dp", scatter_dimension=1, tiled=True
                ).astype(jnp.float32),
                lax.psum_scatter(
                    gradients[5].astype(jnp.bfloat16), "dp", scatter_dimension=1, tiled=True
                ).astype(jnp.float32),
                lax.psum_scatter(
                    gradients[6].astype(jnp.bfloat16), "dp", scatter_dimension=1, tiled=True
                ).astype(jnp.float32),
                lax.psum_scatter(
                    gradients[7].astype(jnp.bfloat16), "dp", scatter_dimension=0, tiled=True
                ).astype(jnp.float32),
            ),
            "seg",
        )
        reduced = (
            lax.psum_scatter(
                lax.psum_scatter(
                    gradients[0].astype(jnp.bfloat16), "dp", scatter_dimension=1, tiled=True
                ),
                "seg",
                scatter_dimension=2,
                tiled=True,
            ).astype(jnp.float32),
            lax.psum_scatter(
                lax.psum_scatter(
                    gradients[1].astype(jnp.bfloat16), "dp", scatter_dimension=1, tiled=True
                ),
                "seg",
                scatter_dimension=2,
                tiled=True,
            ).astype(jnp.float32),
            lax.psum_scatter(
                lax.psum_scatter(
                    gradients[2].astype(jnp.bfloat16), "dp", scatter_dimension=1, tiled=True
                ),
                "seg",
                scatter_dimension=2,
                tiled=True,
            ).astype(jnp.float32),
            lax.psum_scatter(
                lax.psum_scatter(
                    gradients[3].astype(jnp.bfloat16), "dp", scatter_dimension=1, tiled=True
                ),
                "seg",
                scatter_dimension=2,
                tiled=True,
            ).astype(jnp.float32),
            small_sums[0],
            small_sums[1],
            small_sums[2],
            small_sums[3],
        )
        totals = (
            reduced
            if totals is None
            else tuple((jnp.add(earlier, current) for earlier, current in zip(totals, reduced)))
        )
    return (
        jnp.stack(outputs),
        jnp.stack(input_grads),
        totals[0],
        totals[1],
        totals[2],
        totals[3],
        totals[4],
        totals[5],
        totals[6],
        totals[7],
    )


def solution(mesh):
    placed = (
        P(None, "dp", "seg", None),
        P(None, "dp", "seg", None),
        P(None, "dp", None),
        P(None, "dp", None),
        P(None, "dp", "seg"),
        P(None, "dp", "seg"),
        P(None, "dp", "seg"),
        P(None, "dp", "seg"),
        P(None, "dp", None),
        P(None, "dp", None),
        P(None, "dp"),
        P("dp", None),
    )
    return jax.shard_map(
        shards,
        mesh=mesh,
        in_specs=placed,
        out_specs=(
            P(None, "dp", "seg", None),
            P(None, "dp", "seg", None),
            P(None, "dp", "seg"),
            P(None, "dp", "seg"),
            P(None, "dp", "seg"),
            P(None, "dp", "seg"),
            P(None, "dp", None),
            P(None, "dp", None),
            P(None, "dp"),
            P("dp", None),
        ),
        check_vma=False,
    )
```

profile of v0, /device:TPU:0, one launch (start us, length us, event | category | flops | bytes accessed | tf_op | source)
XLA Modules:
  0.0 1764.4 jit_solution(14379314771954475680)
XLA Ops:
  11.2 41.5 %all_gather.32 = bf16[2,96,2304]{1,0,2:T(2,128)(2,1)S(1)} all-gather(bf16[2,96,576]{1,0,2:T(2,128)(2,1)S(1)} %copy.324), channel_id=1, replica_groups=mesh['dp'=8,'seg'=4] {'seg'}, dimensions={2}, use_global_device_ids=true | all-gather | bytes 1105920 | tf_op jit(solution)/shard_map/all_gather | solution.py:226
  55.3 16.7 all_gather.35
  244.1 19.6 %fusion.38 = (u8[128,3072]{1,0:T(8,128)(4,1)S(1)}, u8[128,3072]{1,0:T(8,128)(4,1)S(1)}, u8[128,3072]{1,0:T(8,128)(4,1)S(1)}, u8[128,3072]{1,0:T(8,128)(4,1)S(1)}, f32[8,128,3072]{2,1,0:T(8,128)}) fusion(f32[3072]{0:T(1024)S(1)} %bitcast.509, f32[8,128,3072]{2,1,0:T(8,128)} %fusion.42, bf16[2,768,3072]{2,1,0:T(8,128)(2,1)} %all-gather.14.cloned.1.call-done, ...), kind=kOutput, calls=%fused_computation.141 | convolution fusion | flops 4922277888 | bytes 34629632 | tf_op jit(solution)/shard_map/gld,df->glf/dot_general | solution.py:64
  263.7 61.2 %multiply_convert_fusion.1 = (bf16[8,128,3072]{2,1,0:T(8,128)(2,1)}, f32[8,128,3072]{2,1,0:T(8,128)}, bf16[8,128,3072]{2,1,0:T(8,128)(2,1)}, f32[8,128,3072]{2,1,0:T(8,128)}) fusion(f32[8,128,3072]{2,1,0:T(8,128)} %get-tuple-element.267, f32[3072]{0:T(1024)S(1)} %bitcast.510, u8[128,3072]{1,0:T(8,128)(4,1)S(1)} %get-tuple-element.109, ...), kind=kLoop, calls=%fused_computation.28 | loop fusion | flops 443547648 | bytes 64499712 | tf_op jit(solution)/shard_map/convert_element_type | solution.py:67
  477.5 17.3 fusion.219
  504.6 19.2 %fusion.220 = (bf16[3072]{0:T(1024)(128)(2,1)}, bf16[8,128,3072]{2,1,0:T(8,128)(2,1)}) fusion(f32[8,128,3072]{2,1,0:T(8,128)} %get-tuple-element.203, bf16[8,128,768]{2,1,0:T(8,128)(2,1)} %get-tuple-element.173, bf16[2,3072,768]{2,1,0:T(8,128)(2,1)} %all-gather.18.cloned.1.call-done, f32[8,128,3072]{2,1,0:T(8,128)} %get-tuple-element.267, ...), kind=kOutput, calls=%fused_computation.536 | convolution fusion | flops 4882166784 | bytes 37767168 | tf_op jit(solution)/shard_map/gld,fd->glf/dot_general | solution.py:113
  638.2 18.4 %copy.400 = bf16[2,768,2304]{2,0,1:T(2,128)(2,1)} copy(bf16[2,768,2304]{1,2,0:T(8,128)(2,1)} %pad_maximum_fusion.5) | data formatting | bytes 14155776 | tf_op jit(solution)/shard_map/stack | solution.py:307
  667.4 18.3 %copy.397 = bf16[2,768,2304]{2,0,1:T(2,128)(2,1)} copy(bf16[2,768,2304]{1,2,0:T(8,128)(2,1)} %pad_maximum_fusion.4) | data formatting | bytes 14155776 | tf_op jit(solution)/shard_map/stack | solution.py:307
  800.4 74.9 %all-reduce.10.cloned.1.call-done = (bf16[2,768,2304]{2,0,1:T(2,128)(2,1)}, bf16[2,768,2304]{2,0,1:T(2,128)(2,1)}) async-done(((bf16[2,768,2304]{2,0,1:T(2,128)(2,1)}, bf16[2,768,2304]{2,0,1:T(2,128)(2,1)}), (bf16[2,768,2304]{2,0,1:T(2,128)(2,1)}, bf16[2,768,2304]{2,0,1:T(2,128)(2,1)})) %all-reduce.10.cloned.1.call-update) | async-done | bytes 14155792
  877.1 47.8 %copy.434 = bf16[2,96,2304]{0,1,2:T(8,128)(2,1)} copy(bf16[2,96,2304]{2,0,1:T(2,128)(2,1)S(1)} %constant_dynamic-slice_fusion.1) | data formatting | bytes 1769472
  924.8 83.7 %reshape.972 = bf16[2304,192]{1,0:T(8,128)(2,1)} reshape(bf16[2304,96,2]{2,1,0:T(8,128)(2,1)} %bitcast.442) | data formatting | bytes 1769472
  1010.4 47.8 %copy.436 = bf16[2,96,2304]{0,1,2:T(8,128)(2,1)} copy(bf16[2,96,2304]{2,0,1:T(2,128)(2,1)S(1)} %constant_dynamic-slice_fusion) | data formatting | bytes 1769472
  1058.2 83.7 %reshape.974 = bf16[2304,192]{1,0:T(8,128)(2,1)} reshape(bf16[2304,96,2]{2,1,0:T(8,128)(2,1)} %bitcast.443) | data formatting | bytes 1769472
  1164.1 31.9 %reduce-scatter.49.cloned.1.call-done = bf16[2,96,3072]{2,1,0:T(8,128)(2,1)} async-done(((bf16[2,768,3072]{2,1,0:T(8,128)(2,1)}), bf16[2,96,3072]{2,1,0:T(8,128)(2,1)}) %reduce-scatter.49.cloned.1.call-update) | async-done | bytes 1179664 | tf_op jit(solution)/shard_map/reduce_scatter | solution.py:346
  1216.8 16.4 reduce-scatter.71.cloned.1.call-done
  1234.1 36.2 %reduce-scatter.69.cloned.1.call-done = bf16[96,4]{1,0:T(8,128)(2,1)} async-done(((bf16[768,4]{1,0:T(8,128)(2,1)}), bf16[96,4]{1,0:T(8,128)(2,1)}) %reduce-scatter.69.cloned.1.call-update) | async-done | bytes 784
  1271.2 37.0 %reduce-scatter.79.cloned.1.call-done = bf16[384,2]{1,0:T(8,128)(2,1)} async-done(((bf16[3072,2]{1,0:T(8,128)(2,1)}), bf16[384,2]{1,0:T(8,128)(2,1)}) %reduce-scatter.79.cloned.1.call-update) | async-done | bytes 1552
  1309.2 37.0 %reduce-scatter.77.cloned.1.call-done = bf16[384,2]{1,0:T(8,128)(2,1)} async-done(((bf16[3072,2]{1,0:T(8,128)(2,1)}), bf16[384,2]{1,0:T(8,128)(2,1)}) %reduce-scatter.77.cloned.1.call-update) | async-done | bytes 1552
  1347.2 35.6 %reduce-scatter.75.cloned.1.call-done = bf16[96,12]{1,0:T(8,128)(2,1)} async-done(((bf16[768,12]{1,0:T(8,128)(2,1)}), bf16[96,12]{1,0:T(8,128)(2,1)}) %reduce-scatter.75.cloned.1.call-update) | async-done | bytes 2320
  1383.8 35.8 %reduce-scatter.73.cloned.1.call-done = bf16[96,12]{1,0:T(8,128)(2,1)} async-done(((bf16[768,12]{1,0:T(8,128)(2,1)}), bf16[96,12]{1,0:T(8,128)(2,1)}) %reduce-scatter.73.cloned.1.call-update) | async-done | bytes 2320
  1420.4 35.6 %reduce-scatter.81.cloned.1.call-done = bf16[96,64]{1,0:T(8,128)(2,1)} async-done(((bf16[768,64]{1,0:T(8,128)(2,1)}), bf16[96,64]{1,0:T(8,128)(2,1)}) %reduce-scatter.81.cloned.1.call-update) | async-done | bytes 12304
  1456.9 35.9 %reduce-scatter.83.cloned.1.call-done = bf16[96,64]{1,0:T(8,128)(2,1)} async-done(((bf16[768,64]{1,0:T(8,128)(2,1)}), bf16[96,64]{1,0:T(8,128)(2,1)}) %reduce-scatter.83.cloned.1.call-update) | async-done | bytes 12304
  1493.6 20.4 %all-reduce.4 = (f32[2,96,2]{1,2,0:T(2,128)}, f32[2,96,6]{1,2,0:T(8,128)S(1)}, f32[2,384]{1,0:T(2,128)}, f32[96,64]{0,1:T(8,128)}) all-reduce(f32[2,96,2]{1,2,0:T(2,128)S(1)} %convert_add_fusion.7, f32[2,96,6]{1,2,0:T(8,128)S(1)} %convert_add_fusion.5, f32[2,384]{1,0:T(2,128)S(1)} %convert_add_fusion.6, ...), channel_id=1, replica_groups=mesh['dp'=8,'seg'=4] {'seg'}, use_global_device_ids=true, to_apply=%region_65.66 | all-reduce | flops 8448 | bytes 67584 | tf_op jit(solution)/shard_map/psum | solution.py:311
  1517.8 20.9 %reduce-scatter.65.cloned.1.call-done = bf16[192,192]{1,0:T(8,128)(2,1)} async-done(((bf16[768,192]{1,0:T(8,128)(2,1)}), bf16[192,192]{1,0:T(8,128)(2,1)}) %reduce-scatter.65.cloned.1.call-update) | async-done | bytes 73744
  1540.6 27.9 %reduce-scatter.61.cloned.1.call-done = bf16[576,192]{1,0:T(8,128)(2,1)} async-done(((bf16[2304,192]{1,0:T(8,128)(2,1)}), bf16[576,192]{1,0:T(8,128)(2,1)}) %reduce-scatter.61.cloned.1.call-update) | async-done | bytes 221200
  1568.5 31.4 %reshape.973 = bf16[576,96,2]{2,1,0:T(8,128)(2,1)} reshape(bf16[576,192]{1,0:T(8,128)(2,1)} %reduce-scatter.61.cloned.1.call-done) | data formatting | bytes 442368
  1599.9 14.7 copy.435
  1614.6 31.4 %reshape.975 = bf16[576,96,2]{2,1,0:T(8,128)(2,1)} reshape(bf16[576,192]{1,0:T(8,128)(2,1)} %reduce-scatter.63.cloned.1.call-done) | data formatting | bytes 442368
  1645.9 14.6 copy.437
  1661.4 32.9 %all-reduce.12.cloned.1.call-done = (bf16[2,384,768]{1,0,2:T(2,128)(2,1)}, bf16[2,384,768]{1,0,2:T(2,128)(2,1)}) async-done(((bf16[2,384,768]{1,0,2:T(2,128)(2,1)}, bf16[2,384,768]{1,0,2:T(2,128)(2,1)}), (bf16[2,384,768]{1,0,2:T(2,128)(2,1)}, bf16[2,384,768]{1,0,2:T(2,128)(2,1)})) %all-reduce.12.cloned.1.call-update) | async-done | bytes 2359312
  1696.6 28.4 %reduce-scatter.55.cloned.1.call-done = bf16[2,96,768]{2,1,0:T(8,128)(2,1)} async-done(((bf16[2,96,3072]{2,1,0:T(8,128)(2,1)}), bf16[2,96,768]{2,1,0:T(8,128)(2,1)}) %reduce-scatter.55.cloned.1.call-update) | async-done | bytes 294928 | tf_op jit(solution)/shard_map/reduce_scatter | solution.py:345
  1724.9 30.3 %reduce-scatter.51.cloned.1.call-done = bf16[2,96,768]{2,1,0:T(8,128)(2,1)} async-done(((bf16[2,96,3072]{2,1,0:T(8,128)(2,1)}), bf16[2,96,768]{2,1,0:T(8,128)(2,1)}) %reduce-scatter.51.cloned.1.call-update) | async-done | bytes 294928 | tf_op jit(solution)/shard_map/reduce_scatter | solution.py:345
  (899 shorter events, 640.4 us)
Async XLA Ops:
  7.2 65.9 %all-gather.12.cloned.1.call-start = ((), (), s32[]{:S(2)}) async-start(), calls=%async_computation.22 | async-start | bytes 1474560 | tf_op jit(solution)/shard_map/all_gather | solution.py:232
  7.9 146.0 %all-gather.16.cloned.1.call-start = ((), (), s32[]{:S(2)}) async-start(), calls=%async_computation.24 | async-start | bytes 1474560 | tf_op jit(solution)/shard_map/all_gather | solution.py:235
  10.0 149.2 %all-gather.8.cloned.1.call-start = ((), (), s32[]{:S(2)}) async-start(), calls=%async_computation.20 | async-start | bytes 7962624 | tf_op jit(solution)/shard_map/all_gather | solution.py:225
  55.1 149.8 %all-gather.10.cloned.1.call-start = ((), (), s32[]{:S(2)}) async-start(), calls=%async_computation.21 | async-start | bytes 2654208 | tf_op jit(solution)/shard_map/all_gather | solution.py:228
  73.0 159.9 %all-gather.14.cloned.1.call-start = ((), (), s32[]{:S(2)}) async-start(), calls=%async_computation.23 | async-start | bytes 10616832 | tf_op jit(solution)/shard_map/all_gather | solution.py:231
  73.6 251.4 %all-gather.18.cloned.1.call-start = ((), (), s32[]{:S(2)}) async-start(), calls=%async_computation.25 | async-start | bytes 10616832 | tf_op jit(solution)/shard_map/all_gather | solution.py:234
  148.4 187.0 %copy-start.196 = (f32[768]{0:T(1024)}, f32[768]{0:T(1024)S(1)}, u32[]{:S(2)}) copy-start(f32[768]{0:T(1024)S(1)} %get-tuple-element.156) | copy-start | bytes 9220
  150.3 191.2 %copy-start.110 = (f32[768]{0:T(1024)}, f32[768]{0:T(1024)S(1)}, u32[]{:S(2)}) copy-start(f32[768]{0:T(1024)S(1)} %get-tuple-element.130) | copy-start | bytes 9220
  150.4 220.8 %copy-start.177 = (s32[2,16]{1,0:T(2,128)}, s32[2,16]{1,0:T(2,128)S(1)}, u32[]{:S(2)}) copy-start(s32[2,16]{1,0:T(2,128)S(1)} %get-tuple-element.253) | copy-start | bytes 388
  150.4 225.3 %copy-start.175 = (s32[2,16]{1,0:T(2,128)}, s32[2,16]{1,0:T(2,128)S(1)}, u32[]{:S(2)}) copy-start(s32[2,16]{1,0:T(2,128)S(1)} %get-tuple-element.254) | copy-start | bytes 388
  158.9 635.3 %reduce-scatter.47.cloned.1.call-start = ((), (), s32[]{:S(2)}) async-start(), calls=%async_computation.27 | async-start | bytes 2654208 | tf_op jit(solution)/shard_map/reduce_scatter | solution.py:338
  563.9 232.9 %reduce-scatter.45.cloned.1.call-start = ((), (), s32[]{:S(2)}) async-start(), calls=%async_computation.26 | async-start | bytes 2654208 | tf_op jit(solution)/shard_map/reduce_scatter | solution.py:338
  618.4 256.9 %all-reduce.10.cloned.1.call-start = ((), (), s32[]{:S(2)}) async-start(), calls=%async_computation.46 | async-start | bytes 28311552
  685.8 456.2 %reduce-scatter.59.cloned.1.call-start = ((), (), s32[]{:S(2)}) async-start(), calls=%async_computation.33 | async-start | bytes 10616832 | tf_op jit(solution)/shard_map/reduce_scatter | solution.py:354
  710.4 436.5 %reduce-scatter.57.cloned.1.call-start = ((), (), s32[]{:S(2)}) async-start(), calls=%async_computation.32 | async-start | bytes 10616832 | tf_op jit(solution)/shard_map/reduce_scatter | solution.py:354
  734.4 417.3 %reduce-scatter.53.cloned.1.call-start = ((), (), s32[]{:S(2)}) async-start(), calls=%async_computation.30 | async-start | bytes 10616832 | tf_op jit(solution)/shard_map/reduce_scatter | solution.py:346
  758.1 437.9 %reduce-scatter.49.cloned.1.call-start = ((), (), s32[]{:S(2)}) async-start(), calls=%async_computation.28 | async-start | bytes 10616832 | tf_op jit(solution)/shard_map/reduce_scatter | solution.py:346
  781.5 451.6 %reduce-scatter.71.cloned.1.call-start = ((), (), s32[]{:S(2)}) async-start(), calls=%async_computation.39 | async-start | bytes 221184
  783.9 486.4 %reduce-scatter.69.cloned.1.call-start = ((), (), s32[]{:S(2)}) async-start(), calls=%async_computation.38 | async-start | bytes 221184
  785.3 522.9 %reduce-scatter.79.cloned.1.call-start = ((), (), s32[]{:S(2)}) async-start(), calls=%async_computation.43 | async-start | bytes 884736
  786.8 559.4 %reduce-scatter.77.cloned.1.call-start = ((), (), s32[]{:S(2)}) async-start(), calls=%async_computation.42 | async-start | bytes 884736
  788.5 594.4 %reduce-scatter.75.cloned.1.call-start = ((), (), s32[]{:S(2)}) async-start(), calls=%async_computation.41 | async-start | bytes 221184
  790.2 629.3 %reduce-scatter.73.cloned.1.call-start = ((), (), s32[]{:S(2)}) async-start(), calls=%async_computation.40 | async-start | bytes 221184
  791.6 664.4 %reduce-scatter.81.cloned.1.call-start = ((), (), s32[]{:S(2)}) async-start(), calls=%async_computation.44 | async-start | bytes 221184
  792.9 699.8 %reduce-scatter.83.cloned.1.call-start = ((), (), s32[]{:S(2)}) async-start(), calls=%async_computation.45 | async-start | bytes 221184
  794.2 722.5 %reduce-scatter.67.cloned.1.call-start = ((), (), s32[]{:S(2)}) async-start(), calls=%async_computation.37 | async-start | bytes 491520
  796.8 742.0 %reduce-scatter.65.cloned.1.call-start = ((), (), s32[]{:S(2)}) async-start(), calls=%async_computation.36 | async-start | bytes 491520
  799.1 769.4 %reduce-scatter.61.cloned.1.call-start = ((), (), s32[]{:S(2)}) async-start(), calls=%async_computation.34 | async-start | bytes 1474560
  1008.6 606.0 %reduce-scatter.63.cloned.1.call-start = ((), (), s32[]{:S(2)}) async-start(), calls=%async_computation.35 | async-start | bytes 1474560
  1141.9 552.4 %all-reduce.12.cloned.1.call-start = ((), (), s32[]{:S(2)}) async-start(), calls=%async_computation.47 | async-start | bytes 4718592
  1151.6 573.3 %reduce-scatter.55.cloned.1.call-start = ((), (), s32[]{:S(2)}) async-start(), calls=%async_computation.31 | async-start | bytes 1474560 | tf_op jit(solution)/shard_map/reduce_scatter | solution.py:345
  1152.2 602.9 %reduce-scatter.51.cloned.1.call-start = ((), (), s32[]{:S(2)}) async-start(), calls=%async_computation.29 | async-start | bytes 1474560 | tf_op jit(solution)/shard_map/reduce_scatter | solution.py:345
  (227 other events, 2432.5 us)
Sparse Core Ops, SparseCore 0:
  9.6 46.6 all-gather.11
  58.4 31.0 all-gather.15
  91.9 49.1 all-gather.7
  143.5 28.8 all-gather.9
  174.1 58.6 all-gather.13
  234.6 58.6 all-gather.17
  564.0 42.2 reduce-scatter.46
  618.5 42.4 reduce-scatter.44
  685.9 189.3 all-reduce.9
  878.6 76.7 reduce-scatter.58
  959.0 76.6 reduce-scatter.56
  1039.1 76.6 reduce-scatter.52
  1119.3 76.6 reduce-scatter.48
  1199.5 33.6 reduce-scatter.70
  1236.6 33.6 reduce-scatter.68
  1273.3 34.9 reduce-scatter.78
  1311.3 34.9 reduce-scatter.76
  1349.1 33.6 reduce-scatter.74
  1385.9 33.6 reduce-scatter.72
  1422.4 33.6 reduce-scatter.80
  1459.1 33.6 reduce-scatter.82
  1495.6 21.0 reduce-scatter.66
  1519.6 19.1 reduce-scatter.64
  1540.9 27.5 reduce-scatter.60
  1570.8 27.9 reduce-scatter.62
  1601.0 93.2 all-reduce.11
  1696.5 28.3 reduce-scatter.54
  1727.2 27.9 reduce-scatter.50
where the time goes:
time: 1770 us; the launch traced here: 1760 us
  local copies, waits for them, and re-layouts  541 us (31%)
  waiting for transfers between devices  534 us (30%)
  matrix products  322 us (18%)
  other arithmetic  175 us (10%)
  blocking collectives  171 us (10%)
  between operations  19.8 us (1%)
    unnamed x42, waiting for transfers between devices  430 us
    unnamed x521, local copies, waits for them, and re-layouts  424 us
    convert_element_type x1, other arithmetic, block_forward(): activation = gelu_exact(pre_gelu).astype(jnp.bfloat16)  61.2 us
    reduce_scatter x2, waiting for transfers between devices, shards(): lax.psum_scatter(lax.psum_scatter(gradients[2].astype(jnp.bfloat16), 'dp'...  58.6 us
    another operation x16, other arithmetic, shards(): jnp.stack([local_term, cross_term * first_shard])  44.5 us
    all_gather x1, blocking collectives, shards(): lax.all_gather(project_in, 'seg', axis=2, tiled=True)  41.5 us
    dot_general x4, matrix products, block_backward(): jnp.einsum('gld,fd->glf', branch_grad, down_weight, preferred_element_typ...  41.3 us
    another operation x4, local copies, waits for them, and re-layouts, shards(): jnp.stack([local_term, cross_term * first_shard])  36.7 us
  transfers between devices with their start and end apart: 28, of which 17 were waited for; matrix products, arithmetic and copies ran while one was open for 45% of the time, Pallas kernels for 0%

commit v1 on v0

v1 whole, which is shorter than its diff:
```python
import jax
import jax.numpy as jnp
from jax import lax
from jax.sharding import PartitionSpec as P

HEADS = 12
HD = 64
SEGLEN = 128
POS = 64


NORM_EPS = 1e-05
PRECISE = lax.Precision.HIGHEST


def norm_apply(inputs, norm_gain, norm_shift):
    average = jnp.mean(inputs, axis=-1, keepdims=True)
    centered = inputs - average
    variance = jnp.mean(centered * centered, axis=-1, keepdims=True)
    return centered * lax.rsqrt(variance + NORM_EPS) * norm_gain + norm_shift


def norm_backward(inputs, norm_gain, norm_shift, upstream):
    unused_out, pull_back = jax.vjp(norm_apply, inputs, norm_gain, norm_shift)
    return pull_back(upstream)


def gelu_exact(inputs):
    return jax.nn.gelu(inputs, approximate=False)


def soft_scores(queries, key_rows, same_document):
    scores = jnp.einsum(
        "gqhe,gkhe->ghqk", queries, key_rows, preferred_element_type=jnp.float32
    ) * HD ** (-0.5)
    if same_document is not None:
        scores = jnp.where(same_document[:, None, :, :], scores, -1e30)
    return scores


def block_forward(source, residual, weights, same_document):
    project_in, project_out, up_weight, down_weight, norm_gains, biases, up_bias = weights
    features = source.shape[-1]
    leading = source.shape[:-1]
    head_shape = leading + (HEADS, HD)
    joined = jnp.einsum("gld,de->gle", source, project_in, preferred_element_type=jnp.float32)
    queries = (joined[..., :features] + biases[:, 0]).astype(jnp.bfloat16)
    key_rows = joined[..., features : 2 * features].astype(jnp.bfloat16)
    values = (joined[..., 2 * features :] + biases[:, 1]).astype(jnp.bfloat16)
    scores = soft_scores(queries.reshape(head_shape), key_rows.reshape(head_shape), same_document)
    log_total = jax.nn.logsumexp(scores, axis=-1, keepdims=True)
    attention = jnp.exp(scores - log_total).astype(jnp.bfloat16)
    context = jnp.einsum(
        "ghqk,gkhe->gqhe", attention, values.reshape(head_shape), preferred_element_type=jnp.float32
    )
    context = context.reshape(leading + (features,)).astype(jnp.bfloat16)
    mixed_input = residual + (
        jnp.einsum("gld,de->gle", context, project_out, preferred_element_type=jnp.float32)
        + biases[:, 2]
    )
    first_norm = norm_apply(mixed_input, norm_gains[:, 0], biases[:, 4])
    first_low = first_norm.astype(jnp.bfloat16)
    pre_gelu = (
        jnp.einsum("gld,df->glf", first_low, up_weight, preferred_element_type=jnp.float32)
        + up_bias
    )
    activation = gelu_exact(pre_gelu).astype(jnp.bfloat16)
    second_input = first_norm + (
        jnp.einsum("glf,fd->gld", activation, down_weight, preferred_element_type=jnp.float32)
        + biases[:, 3]
    )
    result = norm_apply(second_input, norm_gains[:, 1], biases[:, 5])
    stored = (
        queries,
        key_rows,
        values,
        log_total,
        context,
        mixed_input,
        first_low,
        pre_gelu,
        activation,
        second_input,
    )
    return (result, stored)


def block_backward(source, stored, weights, same_document, upstream, pick):
    project_in, project_out, up_weight, down_weight, norm_gains, biases, up_bias = weights
    (
        queries,
        key_rows,
        values,
        log_total,
        context,
        mixed_input,
        first_low,
        pre_gelu,
        activation,
        second_input,
    ) = stored
    features = source.shape[-1]
    leading = source.shape[:-1]
    head_shape = leading + (HEADS, HD)
    sum_axes = (0, 1)
    second_grad, gain_two, shift_two = norm_backward(
        second_input, norm_gains[:, 1], biases[:, 5], upstream
    )
    branch_grad = second_grad.astype(jnp.bfloat16)
    down_grad = jnp.einsum(
        "glf,gld->fd", activation, pick(branch_grad), preferred_element_type=jnp.float32
    )
    activation_grad = jnp.einsum(
        "gld,fd->glf", branch_grad, down_weight, preferred_element_type=jnp.float32
    )
    unused_out, gelu_pull = jax.vjp(gelu_exact, pre_gelu)
    pre_gelu_grad = gelu_pull(activation_grad)[0].astype(jnp.bfloat16)
    up_grad = jnp.einsum(
        "gld,glf->df", first_low, pick(pre_gelu_grad), preferred_element_type=jnp.float32
    )
    first_grad = second_grad + jnp.einsum(
        "glf,df->gld", pre_gelu_grad, up_weight, preferred_element_type=jnp.float32
    )
    mixed_grad, gain_one, shift_one = norm_backward(
        mixed_input, norm_gains[:, 0], biases[:, 4], first_grad
    )
    mixed_low = mixed_grad.astype(jnp.bfloat16)
    outward_grad = jnp.einsum("gld,gle->de", context, pick(mixed_low), preferred_element_type=jnp.float32)
    context_grad = jnp.einsum(
        "gle,de->gld", mixed_low, project_out, preferred_element_type=jnp.float32
    )
    context_grad = context_grad.astype(jnp.bfloat16).reshape(head_shape)
    query_heads = queries.reshape(head_shape)
    key_heads = key_rows.reshape(head_shape)
    scores = soft_scores(query_heads, key_heads, same_document)
    attention = jnp.exp(scores - log_total)
    value_grad = jnp.einsum(
        "ghqk,gqhe->gkhe",
        attention.astype(jnp.bfloat16),
        context_grad,
        preferred_element_type=jnp.float32,
    )
    soft_grad = jnp.einsum(
        "gqhe,gkhe->ghqk",
        context_grad,
        values.reshape(head_shape),
        preferred_element_type=jnp.float32,
    )
    score_grad = attention * (soft_grad - jnp.sum(soft_grad * attention, axis=-1, keepdims=True))
    score_grad = score_grad.astype(jnp.bfloat16)
    query_grad = jnp.einsum(
        "ghqk,gkhe->gqhe", score_grad, key_heads, preferred_element_type=jnp.float32
    ) * HD ** (-0.5)
    key_grad = jnp.einsum(
        "ghqk,gqhe->gkhe", score_grad, query_heads, preferred_element_type=jnp.float32
    ) * HD ** (-0.5)
    joined_grad = jnp.concatenate(
        [
            query_grad.reshape(leading + (features,)),
            key_grad.reshape(leading + (features,)),
            value_grad.reshape(leading + (features,)),
        ],
        axis=-1,
    ).astype(jnp.bfloat16)
    inward_grad = jnp.einsum("gld,gle->de", source, pick(joined_grad), preferred_element_type=jnp.float32)
    source_grad = mixed_grad + jnp.einsum(
        "gle,de->gld", joined_grad, project_in, preferred_element_type=jnp.float32
    )
    bias_grad = jnp.stack(
        [
            jnp.sum(joined_grad[..., :features], axis=sum_axes, dtype=jnp.float32),
            jnp.sum(joined_grad[..., 2 * features :], axis=sum_axes, dtype=jnp.float32),
            jnp.sum(mixed_low, axis=sum_axes, dtype=jnp.float32),
            jnp.sum(branch_grad, axis=sum_axes, dtype=jnp.float32),
            shift_one,
            shift_two,
        ],
        axis=-1,
    )
    gain_grad = jnp.stack([gain_one, gain_two], axis=-1)
    bias_up_grad = jnp.sum(pre_gelu_grad, axis=sum_axes, dtype=jnp.float32)
    return (
        source_grad,
        (inward_grad, outward_grad, up_grad, down_grad, gain_grad, bias_grad, bias_up_grad),
    )


def gather_matrix(pieces):
    joined = jnp.concatenate(pieces, axis=1) if len(pieces) > 1 else pieces[0]
    full = lax.all_gather(joined, ("seg", "dp"), axis=0, tiled=False)
    seg = lax.axis_size("seg")
    return full.reshape(seg, -1, joined.shape[1])


def unfold(part):
    return part.transpose(1, 0, 2).reshape(part.shape[1], -1)


def gather_block(project_in, project_out, up_weight, down_weight):
    rows, wide = up_weight.shape
    down_packed = down_weight.reshape(rows, -1)
    first = gather_matrix([project_in, project_out])
    second = gather_matrix([up_weight])
    third = gather_matrix([down_packed])
    seg = third.shape[0]
    down_full = third.reshape(seg, -1, down_weight.shape[1])
    cut = project_in.shape[1]
    return (
        unfold(first[:, :, :cut]),
        unfold(first[:, :, cut:]),
        unfold(second),
        unfold(down_full),
    )


def own_columns(array, shard_index, seg):
    width = array.shape[-1] // seg
    return lax.dynamic_slice_in_dim(array, shard_index * width, width, array.ndim - 1)


def reduce_rows(array):
    return lax.psum_scatter(array.astype(jnp.bfloat16), "dp", scatter_dimension=0, tiled=True)


def reduce_columns(array):
    return lax.psum_scatter(array, "seg", scatter_dimension=1, tiled=True).astype(jnp.float32)


def shards(
    tokens,
    cotangent,
    document_ids,
    position_ids,
    project_in,
    project_out,
    up_weight,
    down_weight,
    norm_gains,
    biases,
    up_bias,
    position_table,
):
    shard_index = lax.axis_index("seg")
    seg = lax.axis_size("seg")
    micro_count, row_count, row_tokens, features = tokens.shape
    segment_count = row_tokens // SEGLEN
    rows = micro_count * row_count
    group_count = rows * segment_count
    own_rows = project_in.shape[1]
    slot_ids = jnp.arange(POS, dtype=jnp.int32)
    up_packed = up_bias.reshape(2, own_rows, -1).transpose(1, 0, 2).reshape(own_rows, -1)
    small = jnp.concatenate(
        [
            norm_gains.transpose(1, 0, 2).reshape(own_rows, 4),
            biases.transpose(1, 0, 2).reshape(own_rows, 12),
            up_packed,
            position_table,
        ],
        axis=1,
    )
    small = lax.all_gather(small, "dp", axis=0, tiled=True)
    many = up_packed.shape[1]
    gains_full = small[:, :4].reshape(features, 2, 2).astype(jnp.float32)
    biases_full = small[:, 4:16].reshape(features, 2, 6).astype(jnp.float32)
    up_full = small[:, 16 : 16 + many].reshape(features, 2, -1).astype(jnp.float32)
    gathered_table = small[:, 16 + many :]

    def weights_of(which):
        return gather_block(
            project_in[which], project_out[which], up_weight[which], down_weight[which]
        ) + (
            gains_full[:, which],
            biases_full[:, which],
            up_full[:, which].reshape(-1),
        )

    local_weights = weights_of(0)
    cross_weights = weights_of(1)
    segments = tokens.reshape(group_count, SEGLEN, features)
    local_out, local_stored = block_forward(
        segments, segments.astype(jnp.float32), local_weights, None
    )
    class_own = local_out[:, 0, :].astype(jnp.bfloat16).reshape(rows, segment_count, features)
    upstream = cotangent.reshape(group_count, SEGLEN, features)
    class_grad_own = upstream[:, 0, :].reshape(rows, segment_count, features)
    class_rows = lax.all_gather(class_own, "seg", axis=1, tiled=True)
    class_grads = lax.all_gather(class_grad_own, "seg", axis=1, tiled=True)
    positions = position_ids.reshape(rows, -1)
    one_hot = (positions[:, :, None] == slot_ids).astype(jnp.bfloat16)
    cross_in = class_rows.astype(jnp.float32) + jnp.einsum(
        "rsp,dp->rsd", one_hot, gathered_table, preferred_element_type=jnp.float32
    )
    documents = document_ids.reshape(rows, -1)
    same_document = documents[:, :, None] == documents[:, None, :]
    cross_low = cross_in.astype(jnp.bfloat16)
    cross_out, cross_stored = block_forward(cross_low, cross_in, cross_weights, same_document)
    cross_own = lax.dynamic_slice_in_dim(cross_out, shard_index * segment_count, segment_count, 1)
    merged = local_out.at[:, 0, :].set(cross_own.reshape(group_count, features))
    layer_out = merged.astype(jnp.bfloat16).reshape(tokens.shape)

    def all_columns(array):
        return array

    def mine(array):
        return own_columns(array, shard_index, seg)

    cross_grad, cross_terms = block_backward(
        cross_low, cross_stored, cross_weights, same_document, class_grads.astype(jnp.float32), mine
    )
    table_grad = jnp.einsum("rsd,rsp->dp", cross_grad, one_hot.astype(jnp.float32), precision=PRECISE)
    own_grad = lax.dynamic_slice_in_dim(cross_grad, shard_index * segment_count, segment_count, 1)
    local_upstream = (
        upstream.astype(jnp.float32).at[:, 0, :].set(own_grad.reshape(group_count, features))
    )
    token_grad, local_terms = block_backward(
        segments, local_stored, local_weights, None, local_upstream, all_columns
    )
    input_grad = token_grad.reshape(tokens.shape)
    cross_packed = reduce_rows(
        jnp.concatenate(
            [
                term.astype(jnp.bfloat16).reshape(features, -1)
                for term in (cross_terms[0], cross_terms[1], cross_terms[2], cross_terms[3])
            ],
            axis=1,
        )
    ).astype(jnp.float32)
    widths = [project_in.shape[2], project_out.shape[2], up_weight.shape[2]]
    ends = [widths[0], widths[0] + widths[1], sum(widths)]
    cross_parts = (
        cross_packed[:, : ends[0]],
        cross_packed[:, ends[0] : ends[1]],
        cross_packed[:, ends[1] : ends[2]],
        cross_packed[:, ends[2] :].reshape(down_weight.shape[1:]),
    )
    local_parts = tuple(reduce_columns(reduce_rows(term)) for term in local_terms[:4])
    matrices = tuple(jnp.stack(pair) for pair in zip(local_parts, cross_parts))

    def small_terms(terms):
        return [terms[4], terms[5], terms[6].reshape(features, -1)]

    first_shard = (shard_index == 0).astype(jnp.float32)
    small_grads = jnp.concatenate(
        small_terms(local_terms)
        + [term * first_shard for term in small_terms(cross_terms) + [table_grad]],
        axis=1,
    )
    small_grads = reduce_rows(small_grads).astype(jnp.float32)
    small_grads = jnp.sum(lax.all_gather(small_grads, "seg", axis=0, tiled=False), axis=0)
    half = many // 2
    local_small = small_grads[:, : 8 + half]
    cross_small = small_grads[:, 8 + half : 16 + many]
    pair = jnp.stack([local_small, cross_small])
    return (layer_out, input_grad) + matrices + (
        pair[:, :, :2],
        pair[:, :, 2:8],
        pair[:, :, 8:].reshape(up_bias.shape),
        small_grads[:, 16 + many :],
    )


def solution(mesh):
    placed = (
        P(None, "dp", "seg", None),
        P(None, "dp", "seg", None),
        P(None, "dp", None),
        P(None, "dp", None),
        P(None, "dp", "seg"),
        P(None, "dp", "seg"),
        P(None, "dp", "seg"),
        P(None, "dp", "seg"),
        P(None, "dp", None),
        P(None, "dp", None),
        P(None, "dp"),
        P("dp", None),
    )
    return jax.shard_map(
        shards,
        mesh=mesh,
        in_specs=placed,
        out_specs=(
            P(None, "dp", "seg", None),
            P(None, "dp", "seg", None),
            P(None, "dp", "seg"),
            P(None, "dp", "seg"),
            P(None, "dp", "seg"),
            P(None, "dp", "seg"),
            P(None, "dp", None),
            P(None, "dp", None),
            P(None, "dp"),
            P("dp", None),
        ),
        check_vma=False,
    )
```

time: 1770 us -> 973 us (0.55)
  local copies, waits for them, and re-layouts: 541 us -> 210 us
  waiting for transfers between devices: 534 us -> 317 us
  blocking collectives: 171 us -> 53.4 us
  matrix products: 322 us -> 244 us
  other arithmetic: 175 us -> 125 us
    unnamed x521 -> x216, local copies, waits for them, and re-layouts: 424 us -> 41.1 us
    unnamed x42 -> x22, waiting for transfers between devices: 430 us -> 132 us
    all_gather x6 -> x2, blocking collectives: 96.1 us -> 24.7 us  [the longest x1 14 us: shards(): lax.all_gather(small_grads, 'seg', axis=0, tiled=False)]
    all_gather x6, waiting for transfers between devices: 12.6 us -> 80.6 us  [gather_matrix(): full = lax.all_gather(joined, ('seg', 'dp'), axis=0, tiled=False)]
    another operation x24 -> x13, other arithmetic: 52 us -> 3.63 us  [the longest x8 2.89 us: shards(): jnp.stack(pair)]
    transpose x0 -> x12, local copies, waits for them, and re-layouts: none -> 47 us  [the longest x10 46.2 us: unfold(): return part.transpose(1, 0, 2).reshape(part.shape[1], -1)]
    reshape x0 -> x11, local copies, waits for them, and re-layouts: none -> 40.8 us  [the longest x2 18.8 us: unfold(): return part.transpose(1, 0, 2).reshape(part.shape[1], -1)]
    psum x1 -> x0, blocking collectives: 20.4 us -> none  [shards(): lax.psum((lax.psum_scatter(gradients[4].astype(jnp.bfloat16), 'dp', scatt...]
  transfers between devices with their start and end apart: 28 -> 16, of which waited for: 17 -> 12; matrix products, arithmetic and copies ran while one was open for 45% -> 41% of each run, Pallas kernels for 0% -> 0%
where the time goes in v1:
time: 973 us; the launch traced here: 966 us
  waiting for transfers between devices  317 us (33%)
  matrix products  244 us (25%)
  local copies, waits for them, and re-layouts  210 us (22%)
  other arithmetic  125 us (13%)
  blocking collectives  53.4 us (5%)
  between operations  16.1 us (2%)
    unnamed x22, waiting for transfers between devices  132 us
    all_gather x6, waiting for transfers between devices, gather_matrix(): full = lax.all_gather(joined, ('seg', 'dp'), axis=0, tiled=False)  80.6 us
    convert_element_type x2, other arithmetic, block_forward(): activation = gelu_exact(pre_gelu).astype(jnp.bfloat16)  62.1 us
    reduce_scatter x1, waiting for transfers between devices, reduce_rows(): lax.psum_scatter(array.astype(jnp.bfloat16), 'dp', scatter_dimension=0, t...  56.3 us
    reduce_scatter x3, waiting for transfers between devices, reduce_columns(): lax.psum_scatter(array, 'seg', scatter_dimension=1, tiled=True)  48.4 us
    transpose x10, local copies, waits for them, and re-layouts, unfold(): return part.transpose(1, 0, 2).reshape(part.shape[1], -1)  46.2 us
    unnamed x216, local copies, waits for them, and re-layouts  41.1 us
    dot_general x2, matrix products, block_backward(): jnp.einsum('gld,fd->glf', branch_grad, down_weight, preferred_element_typ...  32.5 us
  transfers between devices with their start and end apart: 16, of which 12 were waited for; matrix products, arithmetic and copies ran while one was open for 41% of the time, Pallas kernels for 0%

profile of v1, /device:TPU:0, one launch (start us, length us, event | category | flops | bytes accessed | tf_op | source)
XLA Modules:
  0.0 965.9 jit_solution(6642040719359433588)
XLA Ops:
  21.9 10.7 %all-gather.3 = bf16[8,96,88]{1,2,0:T(8,128)(2,1)S(1)} all-gather(bf16[1,96,88]{1,2,0:T(8,128)(2,1)S(1)} %maximum_bitcast_fusion), channel_id=1, replica_groups=mesh['dp'=8,'seg'=4] {'dp'}, dimensions={0}, use_global_device_ids=true | all-gather | bytes 152064 | tf_op jit(solution)/shard_map/all_gather | solution.py:261
  40.9 14.7 %all_gather.52 = bf16[4,16,768]{2,0,1:T(4,128)(2,1)} all-gather(bf16[4,4,768]{2,0,1:T(4,128)(2,1)S(1)} %copy.216), channel_id=1, replica_groups=mesh['dp'=8,'seg'=4] {'seg'}, dimensions={1}, use_global_device_ids=true | all-gather | bytes 122880 | tf_op jit(solution)/shard_map/all_gather | solution.py:287
  56.3 21.5 %all-gather.20.cloned.1.call-done = bf16[3072,768]{1,0:T(8,128)(2,1)} async-done(((bf16[96,768]{1,0:T(8,128)(2,1)}), bf16[3072,768]{1,0:T(8,128)(2,1)}) %all-gather.20.cloned.1.call-update) | async-done | bytes 4718608 | tf_op jit(solution)/shard_map/all_gather | solution.py:190
  89.9 12.2 %convolution_bitcast_fusion = f32[16,128,2304]{1,2,0:T(8,128)} fusion(bf16[768,2304,1]{0,1,2:T(8,128)(2,1)S(1)} %bitcast.265, bf16[16,128,768]{2,1,0:T(8,128)(2,1)} %bitcast.283), kind=kOutput, calls=%fused_computation.28 | convolution fusion | flops 7247757312 | bytes 25559040 | tf_op jit(solution)/shard_map/gld,de->gle/dot_general | solution.py:46
  143.2 8.1 copy.343
  151.3 9.4 reshape.477
  160.6 23.9 %fusion.7 = (u16[128,3072]{1,0:T(8,128)(2,1)S(1)}, u16[128,3072]{1,0:T(8,128)(2,1)S(1)}, f32[16,128,3072]{2,1,0:T(8,128)}) fusion(f32[3072]{0:T(1024)S(1)} %add.280, bf16[768,3072,1]{1,0,2:T(8,128)(2,1)} %reshape.477, f32[16,128,768]{2,1,0:T(8,128)} %copy-done.11, f32[768]{0:T(1024)S(1)} %copy-done.88, f32[768]{0:T(1024)S(1)} %get-tuple-element.175, ...), kind=kOutput, calls=%fused_computation.26 | convolution fusion | flops 9758834688 | bytes 37783552 | tf_op jit(solution)/shard_map/gld,df->glf/dot_general | solution.py:64
  184.6 60.3 %multiply_convert_fusion = (bf16[16,128,3072]{2,1,0:T(8,128)(2,1)}, f32[16,128,3072]{2,1,0:T(8,128)}) fusion(f32[16,128,3072]{2,1,0:T(8,128)} %get-tuple-element.151, f32[3072]{0:T(1024)S(1)} %add.280, u16[128,3072]{1,0:T(8,128)(2,1)S(1)} %get-tuple-element.75, u16[128,3072]{1,0:T(8,128)(2,1)S(1)} %get-tuple-element.74), kind=kLoop, calls=%fused_computation.8 | loop fusion | flops 446693376 | bytes 64499712 | tf_op jit(solution)/shard_map/convert_element_type | solution.py:67
  244.9 11.2 %reshape_reshape.6 = bf16[4,3072,192]{2,1,0:T(8,128)(2,1)} reshape(bf16[32,96,768]{2,1,0:T(8,128)(2,1)} %all-gather.14.cloned.1.call-done) | data formatting | bytes 9437184 | tf_op jit(solution)/shard_map/reshape;reshape | solution.py:206
  264.2 16.2 %fusion.97 = (f32[16,128]{1,0:T(8,128)S(1)}, f32[16,128,768]{2,1,0:T(8,128)S(1)}) fusion(f32[768]{0:T(1024)S(1)} %copy-done.89, bf16[16,128,3072]{2,1,0:T(8,128)(2,1)} %get-tuple-element.123, bf16[3072,768,1]{0,1,2:T(8,128)(2,1)} %bitcast.263, f32[768]{0:T(1024)S(1)} %copy-done.88, f32[768]{0:T(1024)S(1)} %get-tuple-element.175, ...), kind=kOutput, calls=%fused_computation.285 | convolution fusion | flops 9674684416 | bytes 29918208 | tf_op jit(solution)/shard_map/glf,fd->gld/dot_general | solution.py:69
  294.2 14.0 %all_gather.47 = bf16[4,16,768]{2,0,1:T(4,128)(2,1)S(1)} all-gather(bf16[4,4,768]{2,0,1:T(4,128)(2,1)} %copy.200), channel_id=1, replica_groups=mesh['dp'=8,'seg'=4] {'seg'}, dimensions={1}, use_global_device_ids=true | all-gather | bytes 122880 | tf_op jit(solution)/shard_map/all_gather | solution.py:286
  338.6 8.1 copy.342
  346.8 9.4 reshape.482
  357.0 46.3 %all-gather.18.cloned.1.call-done = bf16[32,96,768]{2,1,0:T(8,128)(2,1)} async-done(((bf16[1,96,768]{2,1,0:T(8,128)(2,1)}), bf16[32,96,768]{2,1,0:T(8,128)(2,1)}) %all-gather.18.cloned.1.call-update) | async-done | bytes 4718608 | tf_op jit(solution)/shard_map/all_gather | solution.py:190
  403.4 11.2 %reshape_reshape.7 = bf16[4,3072,192]{2,1,0:T(8,128)(2,1)} reshape(bf16[32,96,768]{2,1,0:T(8,128)(2,1)} %all-gather.18.cloned.1.call-done) | data formatting | bytes 9437184 | tf_op jit(solution)/shard_map/reshape;reshape | solution.py:206
  414.6 8.2 copy.214
  461.9 29.2 %fusion.101 = (bf16[3072]{0:T(1024)(128)(2,1)}, bf16[16,128,3072]{2,1,0:T(8,128)(2,1)}) fusion(f32[16,128,3072]{2,1,0:T(8,128)} %get-tuple-element.124, bf16[16,128,768]{2,1,0:T(8,128)(2,1)S(1)} %get-tuple-element.113, bf16[3072,768,1]{0,1,2:T(8,128)(2,1)} %bitcast.264, f32[16,128,3072]{2,1,0:T(8,128)} %get-tuple-element.151, f32[3072]{0:T(1024)S(1)} %copy-done.73), kind=kOutput, calls=%fused_computation.289 | convolution fusion | flops 9764336640 | bytes 70797312 | tf_op jit(solution)/shard_map/gld,fd->glf/dot_general | solution.py:113
  491.2 19.2 %multiply_reduce_fusion.3 = (bf16[768]{0:T(1024)(128)(2,1)}, f32[16,128]{1,0:T(8,128)S(1)}, bf16[768]{0:T(1024)(128)(2,1)}, f32[16,128,768]{2,1,0:T(8,128)S(1)}) fusion(f32[16,128,768]{2,1,0:T(8,128)} %copy-done.11, f32[16,128]{1,0:T(8,128)S(1)} %copy-done.76, f32[16,128]{1,0:T(8,128)S(1)} %copy-done.65, f32[768]{0:T(1024)S(1)} %copy-done.84, ...), kind=kOutput, calls=%fused_computation.42 | convolution fusion | flops 9679400960 | bytes 36214784 | tf_op jit(solution)/shard_map/glf,df->gld/dot_general | solution.py:121
  527.5 13.6 %multiply_reduce_fusion = (f32[16,12,128]{2,1,0:T(8,128)S(1)}, f32[16,12,128,128]{2,3,1,0:T(8,128)}) fusion(f32[16,12,128,128]{2,3,1,0:T(8,128)} %copy-done, f32[16,12,128]{2,1,0:T(8,128)S(1)} %copy-done.25, bf16[16,128,12,64]{1,3,2,0:T(8,128)(2,1)} %bitcast.246, bf16[16,128,12,64]{1,3,2,0:T(8,128)(2,1)S(1)} %bitcast.245), kind=kOutput, calls=%fused_computation.22 | convolution fusion | flops 415211520 | bytes 31653888 | tf_op jit(solution)/shard_map/gqhe,gkhe->ghqk/dot_general | solution.py:143
  541.1 11.3 %bitcast_reduce_fusion = (bf16[12,64]{1,0:T(8,128)(2,1)}, bf16[16,12,64,128]{3,2,1,0:T(8,128)(2,1)}) fusion(bf16[16,128,12,64]{1,3,2,0:T(8,128)(2,1)S(1)} %bitcast.247, f32[16,12,128,128]{2,3,1,0:T(8,128)} %copy-done, f32[16,12,128]{2,1,0:T(8,128)S(1)} %copy-done.25), kind=kOutput, calls=%fused_computation.68 | convolution fusion | flops 415235328 | bytes 18974208 | tf_op jit(solution)/shard_map/ghqk,gqhe->gkhe/dot_general | solution.py:137
  556.2 10.4 %multiply_convert_fusion.1 = bf16[16,12,128,128]{2,3,1,0:T(8,128)(2,1)S(1)} fusion(f32[16,12,128,128]{2,3,1,0:T(8,128)} %get-tuple-element.166, f32[16,12,128,128]{2,3,1,0:T(8,128)} %copy-done, f32[16,12,128]{2,1,0:T(8,128)S(1)} %get-tuple-element.165, f32[16,12,128]{2,1,0:T(8,128)S(1)} %copy-done.25), kind=kLoop, calls=%fused_computation.21 | loop fusion | flops 15728640 | bytes 31653888 | tf_op jit(solution)/shard_map/convert_element_type | solution.py:150
  585.7 12.3 %fusion.12 = bf16[768,2304]{0,1:T(8,128)(2,1)S(1)} fusion(bf16[16,128,768]{2,1,0:T(8,128)(2,1)} %bitcast.284, bf16[16,128,768]{2,1,0:T(8,128)(2,1)} %copy.238, bf16[16,128,768]{2,1,0:T(8,128)(2,1)} %copy.237, bf16[16,128,768]{2,1,0:T(8,128)(2,1)} %copy.236), kind=kOutput, calls=%fused_computation.60 | convolution fusion | flops 7277838336 | bytes 16121856 | tf_op jit(solution)/shard_map/gld,gle->de/dot_general | solution.py:165
  618.7 16.2 %bitcast_convert_fusion = bf16[3072,768]{1,0:T(8,128)(2,1)} fusion(bf16[16,128,3072]{2,1,0:T(8,128)(2,1)} %get-tuple-element.123, bf16[16,128,768]{2,1,0:T(8,128)(2,1)} %copy-done.33), kind=kOutput, calls=%fused_computation.32 | convolution fusion | flops 9666035712 | bytes 20447232 | tf_op jit(solution)/shard_map/glf,gld->fd/dot_general | solution.py:110
  655.3 18.3 %bitcast_convert_fusion.1 = bf16[768,3072]{1,0:T(8,128)(2,1)} fusion(bf16[16,128,3072]{2,1,0:T(8,128)(2,1)} %get-tuple-element.172, f32[16,128,768]{2,1,0:T(8,128)} %copy-done.11, f32[768]{0:T(1024)} %get-tuple-element.100, f32[768]{0:T(1024)} %copy-done.83, f32[16,128]{1,0:T(8,128)S(1)} %copy-done.76, f32[16,128]{1,0:T(8,128)S(1)} %copy-done.65), kind=kOutput, calls=%fused_computation.33 | convolution fusion | flops 9673900032 | bytes 23615488 | tf_op jit(solution)/shard_map/gld,glf->df/dot_general | solution.py:118
  676.1 12.8 %add_add_fusion.4 = f32[16,128,768]{2,1,0:T(8,128)} fusion(f32[16,128,768]{2,1,0:T(8,128)} %copy-done.12, f32[16,128]{1,0:T(8,128)S(1)} %copy-done.78, bf16[768,2304,1]{0,1,2:T(8,128)(2,1)S(1)} %bitcast.266, bf16[16,128,768]{2,1,0:T(8,128)(2,1)} %copy.238, bf16[16,128,768]{2,1,0:T(8,128)(2,1)} %copy.237, bf16[16,128,768]{2,1,0:T(8,128)(2,1)} %copy.236), kind=kOutput, calls=%fused_computation.53 | convolution fusion | flops 7279214592 | bytes 25567232 | tf_op jit(solution)/shard_map/gle,de->gld/dot_general | solution.py:166
  699.3 56.3 %reduce-scatter.29.cloned.1.call-done = bf16[384,768]{1,0:T(8,128)(2,1)} async-done(((bf16[3072,768]{1,0:T(8,128)(2,1)}), bf16[384,768]{1,0:T(8,128)(2,1)}) %reduce-scatter.29.cloned.1.call-update) | async-done | bytes 589840 | tf_op jit(solution)/shard_map/reduce_scatter | solution.py:222
  757.8 14.0 %all-gather.4 = f32[4,96,88]{1,2,0:T(8,128)S(1)} all-gather(f32[1,96,88]{1,2,0:T(8,128)S(1)} %bitcast_convert_fusion.10), channel_id=4, replica_groups=mesh['dp'=8,'seg'=4] {'seg'}, dimensions={0}, use_global_device_ids=true | all-gather | bytes 168960 | tf_op jit(solution)/shard_map/all_gather | solution.py:349
  779.5 48.1 %reduce-scatter.33.cloned.1.call-done = bf16[96,2304]{1,0:T(8,128)(2,1)} async-done(((bf16[768,2304]{1,0:T(8,128)(2,1)}), bf16[96,2304]{1,0:T(8,128)(2,1)}) %reduce-scatter.33.cloned.1.call-update) | async-done | bytes 442384
  830.3 54.6 %reduce-scatter.37.cloned.1.call-done = bf16[96,3072]{1,0:T(8,128)(2,1)} async-done(((bf16[768,3072]{1,0:T(8,128)(2,1)}), bf16[96,3072]{1,0:T(8,128)(2,1)}) %reduce-scatter.37.cloned.1.call-update) | async-done | bytes 589840
  887.2 22.5 %reduce-scatter.23.cloned.1.call-done = bf16[96,576]{0,1:T(8,128)(2,1)} async-done(((bf16[96,2304]{0,1:T(8,128)(2,1)}), bf16[96,576]{0,1:T(8,128)(2,1)}) %reduce-scatter.23.cloned.1.call-update) | async-done | bytes 110608 | tf_op jit(solution)/shard_map/reduce_scatter | solution.py:226
  911.7 21.3 %reduce-scatter.39.cloned.1.call-done = bf16[192,384]{1,0:T(8,128)(2,1)} async-done(((bf16[768,384]{1,0:T(8,128)(2,1)}), bf16[192,384]{1,0:T(8,128)(2,1)}) %reduce-scatter.39.cloned.1.call-update) | async-done | bytes 147472
  935.3 21.5 %reduce-scatter.27.cloned.1.call-done = bf16[96,768]{0,1:T(8,128)(2,1)} async-done(((bf16[96,3072]{0,1:T(8,128)(2,1)}), bf16[96,768]{0,1:T(8,128)(2,1)}) %reduce-scatter.27.cloned.1.call-update) | async-done | bytes 147472 | tf_op jit(solution)/shard_map/reduce_scatter | solution.py:226
  (452 shorter events, 282.6 us)
Async XLA Ops:
  7.2 26.8 %copy-start.26 = (bf16[2,2,512,768]{3,2,1,0:T(8,128)(2,1)S(1)}, bf16[2,2,512,768]{3,2,1,0:T(8,128)(2,1)}, u32[]{:S(2)}) copy-start(bf16[2,2,512,768]{3,2,1,0:T(8,128)(2,1)} %param.17) | copy-start | bytes 9437188
  7.2 70.6 %all-gather.20.cloned.1.call-start = ((), (), s32[]{:S(2)}) async-start(), calls=%async_computation.18 | async-start | bytes 4866048 | tf_op jit(solution)/shard_map/all_gather | solution.py:190
  10.6 132.6 %all-gather.12.cloned.1.call-start = ((), (), s32[]{:S(2)}) async-start(), calls=%async_computation.10 | async-start | bytes 4866048 | tf_op jit(solution)/shard_map/all_gather | solution.py:190
  12.4 232.5 %all-gather.14.cloned.1.call-start = ((), (), s32[]{:S(2)}) async-start(), calls=%async_computation.11 | async-start | bytes 4866048 | tf_op jit(solution)/shard_map/all_gather | solution.py:190
  16.1 269.4 %all-gather.22.cloned.1.call-start = ((), (), s32[]{:S(2)}) async-start(), calls=%async_computation.19 | async-start | bytes 4866048 | tf_op jit(solution)/shard_map/all_gather | solution.py:190
  17.8 320.8 %all-gather.16.cloned.1.call-start = ((), (), s32[]{:S(2)}) async-start(), calls=%async_computation.12 | async-start | bytes 4866048 | tf_op jit(solution)/shard_map/all_gather | solution.py:190
  18.4 385.0 %all-gather.18.cloned.1.call-start = ((), (), s32[]{:S(2)}) async-start(), calls=%async_computation.13 | async-start | bytes 4866048 | tf_op jit(solution)/shard_map/all_gather | solution.py:190
  18.5 20.1 %copy-start.87 = (s32[2,2,16]{2,1,0:T(2,128)S(1)}, s32[2,2,16]{2,1,0:T(2,128)}, u32[]{:S(2)}) copy-start(s32[2,2,16]{2,1,0:T(2,128)} %param.18) | copy-start | bytes 772
  19.5 627.8 %reduce-scatter.35.cloned.1.call-start = ((), (), s32[]{:S(2)}) async-start(), calls=%async_computation.22 | async-start | bytes 1327104
  32.9 49.2 %copy-start.51 = (bf16[768,88]{0,1:T(8,128)(2,1)}, bf16[768,88]{0,1:T(8,128)(2,1)S(1)}, u32[]{:S(2)}) copy-start(bf16[768,88]{0,1:T(8,128)(2,1)S(1)} %reshape.471) | copy-start | bytes 405508
  37.9 146.6 %copy-start.72 = (f32[3072]{0:T(1024)}, f32[3072]{0:T(1024)S(1)}, u32[]{:S(2)}) copy-start(f32[3072]{0:T(1024)S(1)} %add.280) | copy-start | bytes 36868
  56.3 207.9 %copy-start.83 = (f32[768]{0:T(1024)}, f32[768]{0:T(1024)S(1)}, u32[]{:S(2)}) copy-start(f32[768]{0:T(1024)S(1)} %get-tuple-element.175) | copy-start | bytes 9220
  134.3 129.9 %copy-start.64 = (f32[16,128]{1,0:T(8,128)}, f32[16,128]{1,0:T(8,128)S(1)}, u32[]{:S(2)}) copy-start(f32[16,128]{1,0:T(8,128)S(1)} %broadcast_multiply_fusion.1) | copy-start | bytes 24580
  138.4 125.8 %copy-start.75 = (f32[16,128]{1,0:T(8,128)}, f32[16,128]{1,0:T(8,128)S(1)}, u32[]{:S(2)}) copy-start(f32[16,128]{1,0:T(8,128)S(1)} %fusion.71) | copy-start | bytes 24580
  294.2 33.6 %copy-start.5 = (bf16[768,4,576]{0,2,1:T(8,128)(2,1)}, bf16[768,4,576]{0,2,1:T(8,128)(2,1)S(1)}, u32[]{:S(2)}) copy-start(bf16[768,4,576]{0,2,1:T(8,128)(2,1)S(1)} %copy.202) | copy-start | bytes 10616836
  356.8 81.7 %copy-start.16 = (f32[4,16,768]{2,1,0:T(8,128)}, f32[4,16,768]{2,1,0:T(8,128)S(1)}, u32[]{:S(2)}) copy-start(f32[4,16,768]{2,1,0:T(8,128)S(1)} %get-tuple-element.157) | copy-start | bytes 589828
  356.8 81.7 %copy-start.60 = (f32[4,16]{1,0:T(4,128)}, f32[4,16]{1,0:T(4,128)S(1)}, u32[]{:S(2)}) copy-start(f32[4,16]{1,0:T(4,128)S(1)} %broadcast_multiply_fusion.3) | copy-start | bytes 772
  357.0 81.5 %copy-start.62 = (f32[4,16]{1,0:T(4,128)}, f32[4,16]{1,0:T(4,128)S(1)}, u32[]{:S(2)}) copy-start(f32[4,16]{1,0:T(4,128)S(1)} %fusion.74) | copy-start | bytes 772
  461.9 29.3 %copy-start.33 = (bf16[16,128,768]{2,1,0:T(8,128)(2,1)}, bf16[16,128,768]{2,1,0:T(8,128)(2,1)S(1)}, u32[]{:S(2)}) copy-start(bf16[16,128,768]{2,1,0:T(8,128)(2,1)S(1)} %get-tuple-element.113) | copy-start | bytes 9437188
  461.9 29.3 %copy-start.65 = (f32[16,128]{1,0:T(8,128)S(1)}, f32[16,128]{1,0:T(8,128)}, u32[]{:S(2)}) copy-start(f32[16,128]{1,0:T(8,128)} %copy-done.64) | copy-start | bytes 24580
  461.9 29.3 %copy-start.76 = (f32[16,128]{1,0:T(8,128)S(1)}, f32[16,128]{1,0:T(8,128)}, u32[]{:S(2)}) copy-start(f32[16,128]{1,0:T(8,128)} %copy-done.75) | copy-start | bytes 24580
  461.9 29.3 %copy-start.84 = (f32[768]{0:T(1024)S(1)}, f32[768]{0:T(1024)}, u32[]{:S(2)}) copy-start(f32[768]{0:T(1024)} %copy-done.83) | copy-start | bytes 9220
  491.2 19.2 %copy-start.67 = (f32[16,128]{1,0:T(8,128)S(1)}, f32[16,128]{1,0:T(8,128)}, u32[]{:S(2)}) copy-start(f32[16,128]{1,0:T(8,128)} %copy-done.66) | copy-start | bytes 24580
  575.2 98.6 %reduce-scatter.31.cloned.1.call-start = ((), (), s32[]{:S(2)}) async-start(), calls=%async_computation.20 | async-start | bytes 3981312
  602.1 96.4 %reduce-scatter.41.cloned.1.call-start = ((), (), s32[]{:S(2)}) async-start(), calls=%async_computation.25 | async-start | bytes 221184
  618.7 136.9 %reduce-scatter.29.cloned.1.call-start = ((), (), s32[]{:S(2)}) async-start(), calls=%async_computation.17 | async-start | bytes 5308416 | tf_op jit(solution)/shard_map/reduce_scatter | solution.py:222
  635.0 143.7 %reduce-scatter.25.cloned.1.call-start = ((), (), s32[]{:S(2)}) async-start(), calls=%async_computation.15 | async-start | bytes 245760 | tf_op jit(solution)/shard_map/reduce_scatter | solution.py:226
  649.0 178.6 %reduce-scatter.33.cloned.1.call-start = ((), (), s32[]{:S(2)}) async-start(), calls=%async_computation.21 | async-start | bytes 3981312
  655.3 229.6 %reduce-scatter.37.cloned.1.call-start = ((), (), s32[]{:S(2)}) async-start(), calls=%async_computation.23 | async-start | bytes 5308416
  673.7 236.1 %reduce-scatter.23.cloned.1.call-start = ((), (), s32[]{:S(2)}) async-start(), calls=%async_computation.14 | async-start | bytes 737280 | tf_op jit(solution)/shard_map/reduce_scatter | solution.py:226
  676.0 257.1 %reduce-scatter.39.cloned.1.call-start = ((), (), s32[]{:S(2)}) async-start(), calls=%async_computation.24 | async-start | bytes 737280
  757.7 199.1 %reduce-scatter.27.cloned.1.call-start = ((), (), s32[]{:S(2)}) async-start(), calls=%async_computation.16 | async-start | bytes 983040 | tf_op jit(solution)/shard_map/reduce_scatter | solution.py:226
  (82 other events, 470.7 us)
Sparse Core Ops, SparseCore 0:
  11.5 66.2 all-gather.19
  81.2 61.9 all-gather.11
  146.7 61.9 all-gather.13
  211.4 61.9 all-gather.21
  276.7 61.9 all-gather.15
  341.4 61.9 all-gather.17
  575.3 34.9 reduce-scatter.34
  613.8 47.9 reduce-scatter.30
  664.8 33.6 reduce-scatter.40
  701.7 53.7 reduce-scatter.28
  758.4 20.2 reduce-scatter.24
  782.1 45.5 reduce-scatter.32
  831.1 53.7 reduce-scatter.36
  887.6 22.0 reduce-scatter.22
  912.4 20.5 reduce-scatter.38
  935.2 21.5 reduce-scatter.26

commit v2 on v1

v2 whole, which is shorter than its diff:
```python
import jax
import jax.numpy as jnp
from jax import lax
from jax.sharding import PartitionSpec as P

HEADS = 12
HD = 64
SEGLEN = 128
POS = 64


NORM_EPS = 1e-05
PRECISE = lax.Precision.HIGHEST


def norm_apply(inputs, norm_gain, norm_shift):
    average = jnp.mean(inputs, axis=-1, keepdims=True)
    centered = inputs - average
    variance = jnp.mean(centered * centered, axis=-1, keepdims=True)
    return centered * lax.rsqrt(variance + NORM_EPS) * norm_gain + norm_shift


def norm_backward(inputs, norm_gain, norm_shift, upstream):
    unused_out, pull_back = jax.vjp(norm_apply, inputs, norm_gain, norm_shift)
    return pull_back(upstream)


def gelu_exact(inputs):
    return jax.nn.gelu(inputs, approximate=False)


def soft_scores(queries, key_rows, same_document):
    scores = jnp.einsum(
        "gqhe,gkhe->ghqk", queries, key_rows, preferred_element_type=jnp.float32
    ) * HD ** (-0.5)
    if same_document is not None:
        scores = jnp.where(same_document[:, None, :, :], scores, -1e30)
    return scores


def block_forward(source, residual, weights, same_document):
    project_in, project_out, up_weight, down_weight, norm_gains, biases, up_bias = weights
    features = source.shape[-1]
    leading = source.shape[:-1]
    head_shape = leading + (HEADS, HD)
    joined = jnp.einsum("gld,de->gle", source, project_in, preferred_element_type=jnp.float32)
    queries = (joined[..., :features] + biases[:, 0]).astype(jnp.bfloat16)
    key_rows = joined[..., features : 2 * features].astype(jnp.bfloat16)
    values = (joined[..., 2 * features :] + biases[:, 1]).astype(jnp.bfloat16)
    scores = soft_scores(queries.reshape(head_shape), key_rows.reshape(head_shape), same_document)
    log_total = jax.nn.logsumexp(scores, axis=-1, keepdims=True)
    attention = jnp.exp(scores - log_total).astype(jnp.bfloat16)
    context = jnp.einsum(
        "ghqk,gkhe->gqhe", attention, values.reshape(head_shape), preferred_element_type=jnp.float32
    )
    context = context.reshape(leading + (features,)).astype(jnp.bfloat16)
    mixed_input = residual + (
        jnp.einsum("gld,de->gle", context, project_out, preferred_element_type=jnp.float32)
        + biases[:, 2]
    )
    first_norm = norm_apply(mixed_input, norm_gains[:, 0], biases[:, 4])
    first_low = first_norm.astype(jnp.bfloat16)
    pre_gelu = (
        jnp.einsum("gld,df->glf", first_low, up_weight, preferred_element_type=jnp.float32)
        + up_bias
    )
    activation = gelu_exact(pre_gelu).astype(jnp.bfloat16)
    second_input = first_norm + (
        jnp.einsum("glf,fd->gld", activation, down_weight, preferred_element_type=jnp.float32)
        + biases[:, 3]
    )
    result = norm_apply(second_input, norm_gains[:, 1], biases[:, 5])
    stored = (
        queries,
        key_rows,
        values,
        log_total,
        context,
        mixed_input,
        first_low,
        pre_gelu,
        activation,
        second_input,
    )
    return (result, stored)


def after(value, *earlier):
    return lax.optimization_barrier((value,) + earlier)


def total_over(array, axis_name):
    return jnp.sum(lax.all_gather(array, axis_name, axis=0, tiled=False), axis=0)


def attention_backward(queries, key_rows, values, log_total, same_document, context_grad):
    head_shape = queries.shape[:-1] + (HEADS, HD)
    features = queries.shape[-1]
    leading = queries.shape[:-1]
    context_grad = context_grad.reshape(head_shape)
    query_heads = queries.reshape(head_shape)
    key_heads = key_rows.reshape(head_shape)
    scores = soft_scores(query_heads, key_heads, same_document)
    attention = jnp.exp(scores - log_total)
    value_grad = jnp.einsum(
        "ghqk,gqhe->gkhe",
        attention.astype(jnp.bfloat16),
        context_grad,
        preferred_element_type=jnp.float32,
    )
    soft_grad = jnp.einsum(
        "gqhe,gkhe->ghqk",
        context_grad,
        values.reshape(head_shape),
        preferred_element_type=jnp.float32,
    )
    score_grad = attention * (soft_grad - jnp.sum(soft_grad * attention, axis=-1, keepdims=True))
    score_grad = score_grad.astype(jnp.bfloat16)
    query_grad = jnp.einsum(
        "ghqk,gkhe->gqhe", score_grad, key_heads, preferred_element_type=jnp.float32
    ) * HD ** (-0.5)
    key_grad = jnp.einsum(
        "ghqk,gqhe->gkhe", score_grad, query_heads, preferred_element_type=jnp.float32
    ) * HD ** (-0.5)
    return jnp.concatenate(
        [
            query_grad.reshape(leading + (features,)),
            key_grad.reshape(leading + (features,)),
            value_grad.reshape(leading + (features,)),
        ],
        axis=-1,
    ).astype(jnp.bfloat16)


def local_backward(source, stored, weights, upstream):
    project_in, project_out, up_weight, down_weight, norm_gains, biases, up_bias = weights
    (
        queries,
        key_rows,
        values,
        log_total,
        context,
        mixed_input,
        first_low,
        pre_gelu,
        activation,
        second_input,
    ) = stored
    sum_axes = (0, 1)
    second_grad, gain_two, shift_two = norm_backward(
        second_input, norm_gains[:, 1], biases[:, 5], upstream
    )
    branch_grad = second_grad.astype(jnp.bfloat16)
    down_grad = jnp.einsum(
        "glf,gld->fd", activation, branch_grad, preferred_element_type=jnp.float32
    ).astype(jnp.bfloat16)
    branch_grad, down_grad = after(branch_grad, down_grad)
    activation_grad = jnp.einsum(
        "gld,fd->glf", branch_grad, down_weight, preferred_element_type=jnp.float32
    )
    unused_out, gelu_pull = jax.vjp(gelu_exact, pre_gelu)
    pre_gelu_grad = gelu_pull(activation_grad)[0].astype(jnp.bfloat16)
    up_grad = jnp.einsum(
        "gld,glf->df", first_low, pre_gelu_grad, preferred_element_type=jnp.float32
    ).astype(jnp.bfloat16)
    pre_gelu_grad, up_grad = after(pre_gelu_grad, up_grad)
    first_grad = second_grad + jnp.einsum(
        "glf,df->gld", pre_gelu_grad, up_weight, preferred_element_type=jnp.float32
    )
    mixed_grad, gain_one, shift_one = norm_backward(
        mixed_input, norm_gains[:, 0], biases[:, 4], first_grad
    )
    mixed_low = mixed_grad.astype(jnp.bfloat16)
    outward_grad = jnp.einsum(
        "gld,gle->de", context, mixed_low, preferred_element_type=jnp.float32
    ).astype(jnp.bfloat16)
    mixed_low, outward_grad = after(mixed_low, outward_grad)
    context_grad = jnp.einsum(
        "gle,de->gld", mixed_low, project_out, preferred_element_type=jnp.float32
    ).astype(jnp.bfloat16)
    joined_grad = attention_backward(queries, key_rows, values, log_total, None, context_grad)
    inward_grad = jnp.einsum(
        "gld,gle->de", source, joined_grad, preferred_element_type=jnp.float32
    ).astype(jnp.bfloat16)
    joined_grad, inward_grad = after(joined_grad, inward_grad)
    source_grad = mixed_grad + jnp.einsum(
        "gle,de->gld", joined_grad, project_in, preferred_element_type=jnp.float32
    )
    sums = jnp.sum(joined_grad, axis=sum_axes, dtype=jnp.float32)
    width = source.shape[-1]
    late = jnp.stack([sums[:width], sums[2 * width :]], axis=-1)
    early = jnp.stack(
        [
            jnp.sum(mixed_low, axis=sum_axes, dtype=jnp.float32),
            jnp.sum(branch_grad, axis=sum_axes, dtype=jnp.float32),
            shift_one,
            shift_two,
            gain_one,
            gain_two,
        ],
        axis=-1,
    )
    bias_up_grad = jnp.sum(pre_gelu_grad, axis=sum_axes, dtype=jnp.float32)
    return source_grad, inward_grad, outward_grad, up_grad, down_grad, early, late, bias_up_grad


def dot(left, right):
    return jnp.dot(left, right, preferred_element_type=jnp.float32)


def dot_back(left, right):
    return lax.dot_general(
        left, right, (((1,), (1,)), ((), ())), preferred_element_type=jnp.float32
    )


def dot_weight(left, right):
    return lax.dot_general(
        left, right, (((0,), (0,)), ((), ())), preferred_element_type=jnp.float32
    )


def cross_forward(inputs, weights, same_document, mine):
    project_in, project_out, up_weight, down_weight, norm_gains, biases, up_bias = weights
    rows, length, features = inputs.shape
    flat = inputs.reshape(rows * length, features)
    source = flat.astype(jnp.bfloat16)
    zeros = jnp.zeros((features,), jnp.float32)
    joined_bias = jnp.concatenate([biases[:, 0], zeros, biases[:, 1]])
    joined = (dot(source, project_in) + mine(joined_bias)).astype(jnp.bfloat16)
    joined = lax.all_gather(joined, "seg", axis=1, tiled=True).reshape(rows, length, -1)
    queries = joined[..., :features]
    key_rows = joined[..., features : 2 * features]
    values = joined[..., 2 * features :]
    head_shape = (rows, length, HEADS, HD)
    scores = soft_scores(queries.reshape(head_shape), key_rows.reshape(head_shape), same_document)
    log_total = jax.nn.logsumexp(scores, axis=-1, keepdims=True)
    attention = jnp.exp(scores - log_total).astype(jnp.bfloat16)
    context = jnp.einsum(
        "ghqk,gkhe->gqhe", attention, values.reshape(head_shape), preferred_element_type=jnp.float32
    )
    context = context.reshape(flat.shape).astype(jnp.bfloat16)
    mixed = lax.all_gather(dot(context, project_out), "seg", axis=1, tiled=True)
    mixed_input = flat + (mixed + biases[:, 2])
    first_norm = norm_apply(mixed_input, norm_gains[:, 0], biases[:, 4])
    first_low = first_norm.astype(jnp.bfloat16)
    pre_gelu = dot(first_low, up_weight) + mine(up_bias)
    activation = gelu_exact(pre_gelu).astype(jnp.bfloat16)
    activation = lax.all_gather(activation, "seg", axis=1, tiled=True)
    branch = lax.all_gather(dot(activation, down_weight), "seg", axis=1, tiled=True)
    second_input = first_norm + (branch + biases[:, 3])
    result = norm_apply(second_input, norm_gains[:, 1], biases[:, 5]).reshape(inputs.shape)
    stored = (
        source,
        queries,
        key_rows,
        values,
        log_total,
        context,
        mixed_input,
        first_low,
        pre_gelu,
        activation,
        second_input,
    )
    return result, stored


def cross_backward(stored, weights, same_document, upstream, mine):
    project_in, project_out, up_weight, down_weight, norm_gains, biases, up_bias = weights
    (
        source,
        queries,
        key_rows,
        values,
        log_total,
        context,
        mixed_input,
        first_low,
        pre_gelu,
        activation,
        second_input,
    ) = stored
    features = source.shape[-1]
    second_grad, gain_two, shift_two = norm_backward(
        second_input, norm_gains[:, 1], biases[:, 5], upstream.reshape(source.shape)
    )
    branch_grad = second_grad.astype(jnp.bfloat16)
    branch_mine = mine(branch_grad)
    down_grad = dot_weight(activation, branch_mine)
    partial = dot_back(branch_mine, down_weight)
    seg = lax.axis_size("seg")
    partial = partial.reshape(partial.shape[0], seg, -1).transpose(1, 0, 2)
    partial = lax.all_to_all(partial, "seg", split_axis=0, concat_axis=0, tiled=True)
    activation_grad = jnp.sum(partial, axis=0)
    unused_out, gelu_pull = jax.vjp(gelu_exact, pre_gelu)
    pre_gelu_grad = gelu_pull(activation_grad)[0].astype(jnp.bfloat16)
    up_grad = dot_weight(first_low, pre_gelu_grad)
    first_grad = second_grad + total_over(dot_back(pre_gelu_grad, up_weight), "seg")
    mixed_grad, gain_one, shift_one = norm_backward(
        mixed_input, norm_gains[:, 0], biases[:, 4], first_grad
    )
    mixed_low = mixed_grad.astype(jnp.bfloat16)
    mixed_mine = mine(mixed_low)
    outward_grad = dot_weight(context, mixed_mine)
    context_grad = total_over(dot_back(mixed_mine, project_out), "seg").astype(jnp.bfloat16)
    joined_grad = attention_backward(
        queries, key_rows, values, log_total, same_document, context_grad.reshape(queries.shape)
    ).reshape(source.shape[0], -1)
    joined_mine = mine(joined_grad)
    inward_grad = dot_weight(source, joined_mine)
    source_grad = mixed_grad + total_over(dot_back(joined_mine, project_in), "seg")
    sums = jnp.sum(joined_grad, axis=0, dtype=jnp.float32)
    bias_grad = jnp.stack(
        [
            sums[:features],
            sums[2 * features :],
            jnp.sum(mixed_low, axis=0, dtype=jnp.float32),
            jnp.sum(branch_grad, axis=0, dtype=jnp.float32),
            shift_one,
            shift_two,
            gain_one,
            gain_two,
        ],
        axis=-1,
    )
    bias_up_grad = jnp.sum(pre_gelu_grad, axis=0, dtype=jnp.float32)
    return (
        source_grad.reshape(upstream.shape),
        (inward_grad, outward_grad, up_grad, down_grad),
        bias_grad,
        bias_up_grad,
    )


def pack_rows(pieces, rows):
    return jnp.concatenate([piece.reshape(rows, -1) for piece in pieces], axis=1)


def gather_local(pieces):
    joined = jnp.concatenate(pieces, axis=1)
    full = lax.all_gather(joined, ("seg", "dp"), axis=0, tiled=False)
    return full.reshape(lax.axis_size("seg"), -1, joined.shape[1])


def unfold(part):
    return part.transpose(1, 0, 2).reshape(part.shape[1], -1)


def reduce_rows(array):
    return lax.psum_scatter(array.astype(jnp.bfloat16), "dp", scatter_dimension=0, tiled=True)


def reduce_columns(array):
    return lax.psum_scatter(array, "seg", scatter_dimension=1, tiled=True).astype(jnp.float32)


def shards(
    tokens,
    cotangent,
    document_ids,
    position_ids,
    project_in,
    project_out,
    up_weight,
    down_weight,
    norm_gains,
    biases,
    up_bias,
    position_table,
):
    shard_index = lax.axis_index("seg")
    seg = lax.axis_size("seg")
    micro_count, row_count, row_tokens, features = tokens.shape
    segment_count = row_tokens // SEGLEN
    rows = micro_count * row_count
    group_count = rows * segment_count
    own_rows = project_in.shape[1]
    wide, out_wide, up_wide = project_in.shape[2], project_out.shape[2], up_weight.shape[2]
    slot_ids = jnp.arange(POS, dtype=jnp.int32)

    def mine(array):
        width = array.shape[-1] // seg
        return lax.dynamic_slice_in_dim(array, shard_index * width, width, array.ndim - 1)

    up_packed = up_bias.reshape(2, own_rows, -1).transpose(1, 0, 2).reshape(own_rows, -1)
    many = up_packed.shape[1] // 2
    small = pack_rows(
        [norm_gains.transpose(1, 0, 2), biases.transpose(1, 0, 2), up_packed, position_table],
        own_rows,
    )
    small = lax.all_gather(small, "dp", axis=0, tiled=True)
    gains_full = small[:, :4].reshape(features, 2, 2).astype(jnp.float32)
    biases_full = small[:, 4:16].reshape(features, 2, 6).astype(jnp.float32)
    up_full = small[:, 16 : 16 + 2 * many].reshape(features, 2, -1).astype(jnp.float32)
    gathered_table = small[:, 16 + 2 * many :]

    def vectors(which):
        return gains_full[:, which], biases_full[:, which], up_full[:, which].reshape(-1)

    attend_full = gather_local([project_in[0], project_out[0]])
    feed_full = gather_local([up_weight[0], down_weight[0].reshape(own_rows, -1)])
    local_weights = (
        unfold(attend_full[:, :, :wide]),
        unfold(attend_full[:, :, wide:]),
        unfold(feed_full[:, :, :up_wide]),
        unfold(feed_full[:, :, up_wide:].reshape(seg, -1, down_weight.shape[2])),
    ) + vectors(0)
    cross_full = lax.all_gather(
        pack_rows([project_in[1], project_out[1], up_weight[1], down_weight[1]], own_rows),
        "dp",
        axis=0,
        tiled=True,
    )
    ends = [wide, wide + out_wide, wide + out_wide + up_wide]
    cross_weights = (
        cross_full[:, : ends[0]],
        cross_full[:, ends[0] : ends[1]],
        cross_full[:, ends[1] : ends[2]],
        cross_full[:, ends[2] :].reshape(-1, down_weight.shape[2]),
    ) + vectors(1)

    segments = tokens.reshape(group_count, SEGLEN, features)
    local_out, local_stored = block_forward(
        segments, segments.astype(jnp.float32), local_weights, None
    )
    class_own = local_out[:, 0, :].astype(jnp.bfloat16).reshape(rows, segment_count, features)
    upstream = cotangent.reshape(group_count, SEGLEN, features)
    class_grad_own = upstream[:, 0, :].reshape(rows, segment_count, features)
    class_grads = lax.all_gather(class_grad_own, "seg", axis=1, tiled=True)
    class_rows = lax.all_gather(class_own, "seg", axis=1, tiled=True)
    positions = position_ids.reshape(rows, -1)
    one_hot = (positions[:, :, None] == slot_ids).astype(jnp.bfloat16)
    cross_in = class_rows.astype(jnp.float32) + jnp.einsum(
        "rsp,dp->rsd", one_hot, gathered_table, preferred_element_type=jnp.float32
    )
    documents = document_ids.reshape(rows, -1)
    same_document = documents[:, :, None] == documents[:, None, :]
    cross_out, cross_stored = cross_forward(cross_in, cross_weights, same_document, mine)
    cross_own = lax.dynamic_slice_in_dim(cross_out, shard_index * segment_count, segment_count, 1)
    merged = local_out.at[:, 0, :].set(cross_own.reshape(group_count, features))
    layer_out = merged.astype(jnp.bfloat16).reshape(tokens.shape)

    cross_grad, cross_terms, cross_bias, cross_up = cross_backward(
        cross_stored, cross_weights, same_document, class_grads.astype(jnp.float32), mine
    )
    table_grad = jnp.einsum("rsd,rsp->dp", cross_grad, one_hot.astype(jnp.float32), precision=PRECISE)
    own_grad = lax.dynamic_slice_in_dim(cross_grad, shard_index * segment_count, segment_count, 1)
    local_upstream = (
        upstream.astype(jnp.float32).at[:, 0, :].set(own_grad.reshape(group_count, features))
    )
    cross_packed = reduce_rows(
        pack_rows([term.astype(jnp.bfloat16) for term in cross_terms], features)
    ).astype(jnp.float32)
    token_grad, inward, outward, up_grad, down_grad, early, late, local_up = local_backward(
        segments, local_stored, local_weights, local_upstream
    )
    input_grad = token_grad.reshape(tokens.shape)
    cross_parts = (
        cross_packed[:, : ends[0]],
        cross_packed[:, ends[0] : ends[1]],
        cross_packed[:, ends[1] : ends[2]],
        cross_packed[:, ends[2] :].reshape(down_weight.shape[1:]),
    )
    down_part = reduce_columns(reduce_rows(down_grad))
    up_part = reduce_columns(reduce_rows(up_grad))
    first_shard = (shard_index == 0).astype(jnp.float32)
    pieces = [
        early,
        local_up.reshape(features, -1),
        cross_bias * first_shard,
        cross_up_full(cross_up, shard_index, seg).reshape(features, -1),
        table_grad * first_shard,
    ]
    attend_grads = jnp.concatenate([inward, outward, late.astype(jnp.bfloat16)], axis=1)
    small_grads = reduce_rows(jnp.concatenate(pieces, axis=1)).astype(jnp.float32)
    small_grads = total_over(small_grads, "seg")
    attend_grads = reduce_rows(attend_grads)
    edge = 3 * features
    inward_part = reduce_columns(attend_grads[:, :edge])
    outward_part = reduce_columns(attend_grads[:, edge : edge + features])
    late = total_over(attend_grads[:, edge + features :].astype(jnp.float32), "seg")
    matrices = tuple(
        jnp.stack(pair)
        for pair in zip((inward_part, outward_part, up_part, down_part), cross_parts)
    )
    start = 6 + many
    cross_small = small_grads[:, start : start + 8]
    gains = jnp.stack([small_grads[:, 4:6], cross_small[:, 6:8]])
    bias_out = jnp.stack(
        [jnp.concatenate([late, small_grads[:, :4]], axis=1), cross_small[:, :6]]
    )
    ups = jnp.stack(
        [small_grads[:, 6:start], small_grads[:, start + 8 : start + 8 + many]]
    ).reshape(up_bias.shape)
    return (layer_out, input_grad) + matrices + (
        gains,
        bias_out,
        ups,
        small_grads[:, start + 8 + many :],
    )


def cross_up_full(own, shard_index, seg):
    full = jnp.zeros((own.shape[0] * seg,), own.dtype)
    return lax.dynamic_update_slice_in_dim(full, own, shard_index * own.shape[0], 0)


def solution(mesh):
    placed = (
        P(None, "dp", "seg", None),
        P(None, "dp", "seg", None),
        P(None, "dp", None),
        P(None, "dp", None),
        P(None, "dp", "seg"),
        P(None, "dp", "seg"),
        P(None, "dp", "seg"),
        P(None, "dp", "seg"),
        P(None, "dp", None),
        P(None, "dp", None),
        P(None, "dp"),
        P("dp", None),
    )
    return jax.shard_map(
        shards,
        mesh=mesh,
        in_specs=placed,
        out_specs=(
            P(None, "dp", "seg", None),
            P(None, "dp", "seg", None),
            P(None, "dp", "seg"),
            P(None, "dp", "seg"),
            P(None, "dp", "seg"),
            P(None, "dp", "seg"),
            P(None, "dp", None),
            P(None, "dp", None),
            P(None, "dp"),
            P("dp", None),
        ),
        check_vma=False,
    )
```

time: 973 us -> 1100 us (1.13)
  blocking collectives: 53.4 us -> 172 us
  local copies, waits for them, and re-layouts: 210 us -> 179 us
  waiting for transfers between devices: 317 us -> 345 us
  other arithmetic: 125 us -> 139 us
  matrix products: 244 us -> 233 us
    all_gather x1 -> x9, blocking collectives: 14 us -> 134 us  [the longest x5 76.4 us: total_over(): lax.all_gather(array, axis_name, axis=0, tiled=False)]
    reduce_scatter x1 -> x3, waiting for transfers between devices: 56.3 us -> 145 us  [reduce_rows(): lax.psum_scatter(array.astype(jnp.bfloat16), 'dp', scatter_dimension=0, t...]
    unnamed x22 -> x17, waiting for transfers between devices: 132 us -> 84.7 us
    reduce_scatter x3 -> x1, waiting for transfers between devices: 48.4 us -> 20.5 us  [reduce_columns(): lax.psum_scatter(array, 'seg', scatter_dimension=1, tiled=True)]
    concatenate x2 -> x8, local copies, waits for them, and re-layouts: 0.21 us -> 27.2 us  [the longest x1 19.4 us: shards(): jnp.concatenate([inward, outward, late.astype(jnp.bfloat16)], axis=1)]
    another operation x24 -> x26, local copies, waits for them, and re-layouts: 34 us -> 9.52 us  [the longest x9 4.61 us: cross_backward(): jnp.stack([sums[:features], sums[2 * features:], jnp.sum(mixed_low, axis=...]
    reshape x18 -> x11, local copies, waits for them, and re-layouts: 37.8 us -> 16.8 us  [the longest x1 11.2 us: shards(): feed_full[:, :, up_wide:].reshape(seg, -1, down_weight.shape[2])]
    transpose x10 -> x6, local copies, waits for them, and re-layouts: 46.2 us -> 29.7 us  [unfold(): return part.transpose(1, 0, 2).reshape(part.shape[1], -1)]
  transfers between devices with their start and end apart: 16 -> 13, of which waited for: 12 -> 12; matrix products, arithmetic and copies ran while one was open for 41% -> 13% of each run, Pallas kernels for 0% -> 0%
where the time goes in v2:
time: 1100 us; the launch traced here: 1090 us
  waiting for transfers between devices  345 us (31%)
  matrix products  233 us (21%)
  local copies, waits for them, and re-layouts  179 us (16%)
  blocking collectives  172 us (16%)
  other arithmetic  139 us (13%)
  between operations  16.3 us (1%)
    reduce_scatter x3, waiting for transfers between devices, reduce_rows(): lax.psum_scatter(array.astype(jnp.bfloat16), 'dp', scatter_dimension=0, t...  145 us
    unnamed x17, waiting for transfers between devices  84.7 us
    all_gather x2, waiting for transfers between devices, gather_local(): full = lax.all_gather(joined, ('seg', 'dp'), axis=0, tiled=False)  81.6 us
    all_gather x5, blocking collectives, total_over(): lax.all_gather(array, axis_name, axis=0, tiled=False)  76.4 us
    convert_element_type x1, other arithmetic, block_forward(): activation = gelu_exact(pre_gelu).astype(jnp.bfloat16)  60.3 us
    unnamed x212, local copies, waits for them, and re-layouts  48.8 us
    transpose x6, local copies, waits for them, and re-layouts, unfold(): return part.transpose(1, 0, 2).reshape(part.shape[1], -1)  29.7 us
    dot_general x1, matrix products, local_backward(): jnp.einsum('gld,fd->glf', branch_grad, down_weight, preferred_element_typ...  27.4 us
  transfers between devices with their start and end apart: 13, of which 12 were waited for; matrix products, arithmetic and copies ran while one was open for 13% of the time, Pallas kernels for 0%

profile of v2, /device:TPU:0, one launch (start us, length us, event | category | flops | bytes accessed | tf_op | source)
XLA Modules:
  0.0 1089.5 jit_solution(226094634697774237)
XLA Ops:
  30.6 13.8 %all_gather.83 = bf16[4,16,768]{2,0,1:T(4,128)(2,1)S(1)} all-gather(bf16[4,4,768]{2,0,1:T(4,128)(2,1)S(1)} %copy.306), channel_id=1, replica_groups=mesh['dp'=8,'seg'=4] {'seg'}, dimensions={1}, use_global_device_ids=true | all-gather | bytes 122880 | tf_op jit(solution)/shard_map/all_gather | solution.py:430
  55.7 60.7 %all-gather.19.cloned.1.call-done = bf16[3072,768]{1,0:T(8,128)(2,1)} async-done(((bf16[96,768]{1,0:T(8,128)(2,1)}), bf16[3072,768]{1,0:T(8,128)(2,1)}) %all-gather.19.cloned.1.call-update) | async-done | bytes 4718608 | tf_op jit(solution)/shard_map/all_gather | solution.py:342
  178.8 21.0 %all-gather.21.cloned.1.call-done = bf16[3072,1536]{1,0:T(8,128)(2,1)} async-done(((bf16[96,1536]{1,0:T(8,128)(2,1)}), bf16[3072,1536]{1,0:T(8,128)(2,1)}) %all-gather.21.cloned.1.call-update) | async-done | bytes 9437200 | tf_op jit(solution)/shard_map/all_gather | solution.py:342
  240.8 24.2 %fusion.7 = (u16[128,3072]{1,0:T(8,128)(2,1)S(1)}, u16[128,3072]{1,0:T(8,128)(2,1)S(1)}, f32[16,128,3072]{2,1,0:T(8,128)}) fusion(f32[3072]{0:T(1024)S(1)} %add.266, bf16[768,3072,1]{1,0,2:T(8,128)(2,1)} %reshape.490, f32[16,128,768]{2,1,0:T(8,128)} %copy-done.9, f32[768]{0:T(1024)S(1)} %copy-done.79, f32[768]{0:T(1024)S(1)} %copy-done.67, ...), kind=kOutput, calls=%fused_computation.26 | convolution fusion | flops 9758834688 | bytes 37783552 | tf_op jit(solution)/shard_map/gld,df->glf/dot_general | solution.py:64
  265.0 60.3 %multiply_convert_fusion = (bf16[16,128,3072]{2,1,0:T(8,128)(2,1)}, f32[16,128,3072]{2,1,0:T(8,128)}) fusion(f32[16,128,3072]{2,1,0:T(8,128)} %get-tuple-element.196, f32[3072]{0:T(1024)S(1)} %add.266, u16[128,3072]{1,0:T(8,128)(2,1)S(1)} %get-tuple-element.111, u16[128,3072]{1,0:T(8,128)(2,1)S(1)} %get-tuple-element.110), kind=kLoop, calls=%fused_computation.8 | loop fusion | flops 446693376 | bytes 64499712 | tf_op jit(solution)/shard_map/convert_element_type | solution.py:67
  325.4 15.4 %fusion.100 = (f32[16,128]{1,0:T(8,128)S(1)}, f32[16,128,768]{2,1,0:T(8,128)S(1)}) fusion(f32[768]{0:T(1024)S(1)} %copy-done.80, bf16[16,128,3072]{2,1,0:T(8,128)(2,1)} %get-tuple-element.160, bf16[3072,768,1]{0,1,2:T(8,128)(2,1)} %bitcast.275, f32[768]{0:T(1024)S(1)} %copy-done.79, f32[768]{0:T(1024)S(1)} %copy-done.67, f32[16,128]{1,0:T(8,128)S(1)} %fusion.68, ...), kind=kOutput, calls=%fused_computation.283 | convolution fusion | flops 9674684416 | bytes 29918208 | tf_op jit(solution)/shard_map/glf,fd->gld/dot_general | solution.py:69
  345.4 13.3 %all_gather.77 = bf16[4,16,768]{2,0,1:T(4,128)(2,1)S(1)} all-gather(bf16[4,4,768]{2,0,1:T(4,128)(2,1)S(1)} %copy.294), channel_id=1, replica_groups=mesh['dp'=8,'seg'=4] {'seg'}, dimensions={1}, use_global_device_ids=true | all-gather | bytes 122880 | tf_op jit(solution)/shard_map/all_gather | solution.py:431
  361.0 14.0 %all-gather.8 = bf16[4,576,64]{1,2,0:T(8,128)(2,1)S(1)} all-gather(bf16[1,576,64]{1,2,0:T(8,128)(2,1)S(1)} %fusion.23), channel_id=1, replica_groups=mesh['dp'=8,'seg'=4] {'seg'}, dimensions={0}, use_global_device_ids=true | all-gather | bytes 368640 | tf_op jit(solution)/shard_map/all_gather | solution.py:231
  378.9 13.8 %all-gather.9 = f32[4,192,64]{1,2,0:T(8,128)S(1)} all-gather(f32[1,192,64]{1,2,0:T(8,128)S(1)} %convolution_bitcast_fusion.4), channel_id=1, replica_groups=mesh['dp'=8,'seg'=4] {'seg'}, dimensions={0}, use_global_device_ids=true | all-gather | bytes 245760 | tf_op jit(solution)/shard_map/all_gather | solution.py:243
  396.2 14.9 %all_gather.81 = bf16[64,3072]{1,0:T(8,128)(2,1)S(1)} all-gather(bf16[64,768]{1,0:T(8,128)(2,1)S(1)} %get-tuple-element.156), channel_id=1, replica_groups=mesh['dp'=8,'seg'=4] {'seg'}, dimensions={1}, use_global_device_ids=true | all-gather | bytes 491520 | tf_op jit(solution)/shard_map/all_gather | solution.py:249
  413.7 14.4 %all-gather.10 = f32[4,192,64]{1,2,0:T(8,128)S(1)} all-gather(f32[1,192,64]{1,2,0:T(8,128)S(1)} %convolution_bitcast_fusion.3), channel_id=1, replica_groups=mesh['dp'=8,'seg'=4] {'seg'}, dimensions={0}, use_global_device_ids=true | all-gather | bytes 245760 | tf_op jit(solution)/shard_map/all_gather | solution.py:250
  441.1 14.1 %all-to-all-done = f32[4,64,768]{2,1,0:T(8,128)S(1)} async-done(((f32[4,64,768]{2,1,0:T(8,128)}), f32[4,64,768]{2,1,0:T(8,128)S(1)}, u32[]{:S(2)}, u32[]{:S(2)}) %all-to-all-start) | async-done | bytes 786464 | tf_op jit(solution)/shard_map/all_to_all | solution.py:294
  458.3 18.1 %all-gather.2 = f32[256,768]{1,0:T(8,128)S(1)} all-gather(f32[64,768]{1,0:T(8,128)S(1)} %fusion.24), channel_id=4, replica_groups=mesh['dp'=8,'seg'=4] {'seg'}, dimensions={0}, use_global_device_ids=true | all-gather | bytes 983040 | tf_op jit(solution)/shard_map/all_gather | solution.py:93
  480.2 18.2 %all-gather.3 = f32[256,768]{1,0:T(8,128)S(1)} all-gather(f32[64,768]{1,0:T(8,128)S(1)} %fusion.32), channel_id=5, replica_groups=mesh['dp'=8,'seg'=4] {'seg'}, dimensions={0}, use_global_device_ids=true | all-gather | bytes 983040 | tf_op jit(solution)/shard_map/all_gather | solution.py:93
  502.9 15.6 %all-gather.4 = f32[256,768]{1,0:T(8,128)S(1)} all-gather(f32[64,768]{1,0:T(8,128)S(1)} %fusion.27), channel_id=6, replica_groups=mesh['dp'=8,'seg'=4] {'seg'}, dimensions={0}, use_global_device_ids=true | all-gather | bytes 983040 | tf_op jit(solution)/shard_map/all_gather | solution.py:93
  536.3 12.1 %bitcast_convert_fusion.1 = bf16[3072,768]{1,0:T(8,128)(2,1)} fusion(bf16[16,128,3072]{2,1,0:T(8,128)(2,1)S(1)} %bitcast.271, bf16[16,128,768]{2,1,0:T(8,128)(2,1)S(1)} %add_convert_fusion.2), kind=kOutput, calls=%fused_computation.33 | convolution fusion | flops 9666035712 | bytes 20447232 | tf_op jit(solution)/shard_map/glf,gld->fd/dot_general | solution.py:154
  548.4 27.4 %add_convert_fusion = bf16[16,128,3072]{2,1,0:T(8,128)(2,1)} fusion(f32[16,128,3072]{2,1,0:T(8,128)} %get-tuple-element.161, f32[16,128,3072]{2,1,0:T(8,128)} %get-tuple-element.196, f32[3072]{0:T(1024)S(1)} %add.266, bf16[16,128,768]{2,1,0:T(8,128)(2,1)S(1)} %add_convert_fusion.2, bf16[3072,768,1]{0,1,2:T(8,128)(2,1)} %bitcast.276), kind=kOutput, calls=%fused_computation.7 | convolution fusion | flops 9758048256 | bytes 70791168 | tf_op jit(solution)/shard_map/gld,fd->glf/dot_general | solution.py:158
  575.9 18.2 %bitcast_convert_fusion = bf16[768,3072]{1,0:T(8,128)(2,1)} fusion(bf16[16,128,3072]{2,1,0:T(8,128)(2,1)} %add_convert_fusion, f32[16,128,768]{2,1,0:T(8,128)} %copy-done.9, f32[768]{0:T(1024)S(1)} %copy-done.79, f32[768]{0:T(1024)S(1)} %copy-done.67, f32[16,128]{1,0:T(8,128)S(1)} %fusion.68, f32[16,128]{1,0:T(8,128)S(1)} %broadcast_multiply_fusion.1), kind=kOutput, calls=%fused_computation.32 | convolution fusion | flops 9673900032 | bytes 23615488 | tf_op jit(solution)/shard_map/gld,glf->df/dot_general | solution.py:163
  594.1 20.9 %multiply_reduce_fusion.3 = (bf16[768]{0:T(1024)(128)(2,1)}, f32[16,128]{1,0:T(8,128)S(1)}, bf16[768]{0:T(1024)(128)(2,1)}, f32[16,128,768]{2,1,0:T(8,128)}) fusion(f32[16,128,768]{2,1,0:T(8,128)} %copy-done.9, f32[16,128]{1,0:T(8,128)S(1)} %fusion.68, f32[16,128]{1,0:T(8,128)S(1)} %broadcast_multiply_fusion.1, f32[768]{0:T(1024)S(1)} %copy-done.67, ...), kind=kOutput, calls=%fused_computation.42 | convolution fusion | flops 9679400960 | bytes 36214784 | tf_op jit(solution)/shard_map/glf,df->gld/dot_general | solution.py:167
  635.0 14.6 %multiply_reduce_fusion = (f32[16,12,128]{2,1,0:T(8,128)S(1)}, f32[16,12,128,128]{2,3,1,0:T(8,128)}) fusion(f32[16,12,128,128]{2,3,1,0:T(8,128)} %copy-done, f32[16,12,128]{2,1,0:T(8,128)S(1)} %copy-done.28, bf16[16,128,12,64]{1,3,2,0:T(8,128)(2,1)S(1)} %bitcast.255, bf16[16,128,12,64]{1,3,2,0:T(8,128)(2,1)} %bitcast.257), kind=kOutput, calls=%fused_computation.22 | convolution fusion | flops 415211520 | bytes 31653888 | tf_op jit(solution)/shard_map/gqhe,gkhe->ghqk/dot_general | solution.py:111
  679.5 15.6 %fusion.12 = bf16[768,2304]{0,1:T(8,128)(2,1)} fusion(bf16[16,128,768]{2,1,0:T(8,128)(2,1)} %bitcast.308, bf16[16,128,768]{1,2,0:T(8,128)(2,1)} %bitcast.266, bf16[16,128,768]{1,2,0:T(8,128)(2,1)} %bitcast.268, bf16[16,128,768]{1,2,0:T(8,128)(2,1)} %bitcast.259), kind=kOutput, calls=%fused_computation.59 | convolution fusion | flops 7277838336 | bytes 16121856 | tf_op jit(solution)/shard_map/gld,gle->de/dot_general | solution.py:182
  705.1 19.4 %concatenate.59 = bf16[768,3074]{0,1:T(8,128)(2,1)} concatenate(bf16[768,2304]{0,1:T(8,128)(2,1)} %fusion.12, bf16[768,768]{0,1:T(8,128)(2,1)S(1)} %copy.328, bf16[768,1]{0,1:T(2,128)(2,1)S(1)} %stack.133, bf16[768,1]{0,1:T(2,128)(2,1)S(1)} %stack.134), dimensions={1} | concatenate | bytes 9443328 | tf_op jit(solution)/shard_map/concatenate | solution.py:475
  773.3 12.6 %reduce-scatter.28.cloned.1.call-done = bf16[96,3074]{1,0:T(8,128)(2,1)} async-done(((bf16[768,3074]{1,0:T(8,128)(2,1)}), bf16[96,3074]{1,0:T(8,128)(2,1)}) %reduce-scatter.28.cloned.1.call-update) | async-done | bytes 590224
  792.1 14.2 %add_add_fusion.4 = f32[16,128,768]{2,1,0:T(8,128)} fusion(f32[16,128,768]{2,1,0:T(8,128)} %copy-done.10, f32[16,128]{1,0:T(8,128)S(1)} %negate_multiply_fusion.2, bf16[16,128,2304]{1,2,0:T(8,128)(2,1)} %pad_maximum_fusion, bf16[768,2304,1]{0,1,2:T(8,128)(2,1)} %bitcast.278), kind=kOutput, calls=%fused_computation.53 | convolution fusion | flops 7250903040 | bytes 25567232 | tf_op jit(solution)/shard_map/gle,de->gld/dot_general | solution.py:186
  806.3 16.8 %reduce-scatter.36.cloned.1.call-done = bf16[96,86]{1,0:T(8,128)(2,1)} async-done(((bf16[768,86]{1,0:T(8,128)(2,1)}), bf16[96,86]{1,0:T(8,128)(2,1)}) %reduce-scatter.36.cloned.1.call-update) | async-done | bytes 16528
  823.9 13.6 %all-gather.11 = f32[4,96,86]{1,2,0:T(8,128)S(1)} all-gather(f32[1,96,86]{1,2,0:T(8,128)S(1)} %bitcast_convert_fusion.9), channel_id=7, replica_groups=mesh['dp'=8,'seg'=4] {'seg'}, dimensions={0}, use_global_device_ids=true | all-gather | bytes 165120 | tf_op jit(solution)/shard_map/all_gather | solution.py:93
  837.5 42.7 %reduce-scatter.26.cloned.1.call-done = bf16[384,768]{1,0:T(8,128)(2,1)} async-done(((bf16[3072,768]{1,0:T(8,128)(2,1)}), bf16[384,768]{1,0:T(8,128)(2,1)}) %reduce-scatter.26.cloned.1.call-update) | async-done | bytes 589840 | tf_op jit(solution)/shard_map/reduce_scatter | solution.py:351
  884.6 47.0 %reduce-scatter.20.cloned.1.call-done = bf16[96,2304]{1,0:T(8,128)(2,1)} async-done(((bf16[768,2304]{1,0:T(8,128)(2,1)}), bf16[96,2304]{1,0:T(8,128)(2,1)}) %reduce-scatter.20.cloned.1.call-update) | async-done | bytes 442384 | tf_op jit(solution)/shard_map/reduce_scatter | solution.py:351
  933.9 54.9 %reduce-scatter.22.cloned.1.call-done = bf16[96,3072]{1,0:T(8,128)(2,1)} async-done(((bf16[768,3072]{1,0:T(8,128)(2,1)}), bf16[96,3072]{1,0:T(8,128)(2,1)}) %reduce-scatter.22.cloned.1.call-update) | async-done | bytes 589840 | tf_op jit(solution)/shard_map/reduce_scatter | solution.py:351
  1012.9 21.6 %reduce-scatter.30.cloned.1.call-done = bf16[576,96]{1,0:T(8,128)(2,1)} async-done(((bf16[2304,96]{1,0:T(8,128)(2,1)}), bf16[576,96]{1,0:T(8,128)(2,1)}) %reduce-scatter.30.cloned.1.call-update) | async-done | bytes 110608
  1036.4 21.5 %reduce-scatter.34.cloned.1.call-done = bf16[192,384]{1,0:T(8,128)(2,1)} async-done(((bf16[768,384]{1,0:T(8,128)(2,1)}), bf16[192,384]{1,0:T(8,128)(2,1)}) %reduce-scatter.34.cloned.1.call-update) | async-done | bytes 147472
  1060.1 20.5 %reduce-scatter.24.cloned.1.call-done = bf16[96,768]{1,0:T(8,128)(2,1)} async-done(((bf16[96,3072]{1,0:T(8,128)(2,1)}), bf16[96,768]{1,0:T(8,128)(2,1)}) %reduce-scatter.24.cloned.1.call-update) | async-done | bytes 147472 | tf_op jit(solution)/shard_map/reduce_scatter | solution.py:355
  (480 shorter events, 347.9 us)
Async XLA Ops:
  7.2 41.7 %copy-start.75 = (s32[2,2,16]{2,1,0:T(2,128)S(1)}, s32[2,2,16]{2,1,0:T(2,128)}, u32[]{:S(2)}) copy-start(s32[2,2,16]{2,1,0:T(2,128)} %param.18) | copy-start | bytes 772
  7.2 42.4 %all-gather.17.cloned.1.call-start = ((), (), s32[]{:S(2)}) async-start(), calls=%async_computation.10 | async-start | bytes 3981312 | tf_op jit(solution)/shard_map/all_gather | solution.py:409
  12.3 104.0 %all-gather.19.cloned.1.call-start = ((), (), s32[]{:S(2)}) async-start(), calls=%async_computation.15 | async-start | bytes 4866048 | tf_op jit(solution)/shard_map/all_gather | solution.py:342
  13.2 186.6 %all-gather.21.cloned.1.call-start = ((), (), s32[]{:S(2)}) async-start(), calls=%async_computation.16 | async-start | bytes 9732096 | tf_op jit(solution)/shard_map/all_gather | solution.py:342
  232.6 92.8 %slice-start.5 = ((s8[6291456]{0:T(1024)(128)(4,1)}), s8[2097152]{0:T(1024)(128)(4,1)S(1)}, s32[]{:S(2)}) async-start(s8[6291456]{0:T(1024)(128)(4,1)} %bitcast.261), calls=%async_computation.27 | async-start | bytes 4194304
  240.8 84.6 %slice-start.6 = ((s8[6291456]{0:T(1024)(128)(4,1)}), s8[4194304]{0:T(1024)(128)(4,1)S(1)}, s32[]{:S(2)}) async-start(s8[6291456]{0:T(1024)(128)(4,1)} %bitcast.261), calls=%async_computation.28 | async-start | bytes 8388608
  265.0 60.4 %copy-start.80 = (f32[768]{0:T(1024)S(1)}, f32[768]{0:T(1024)}, u32[]{:S(2)}) copy-start(f32[768]{0:T(1024)} %get-tuple-element.130) | copy-start | bytes 9220
  341.7 34.4 %copy-start.76 = (pred[4,16,16]{1,2,0:T(8,128)(4,1)S(1)}, pred[4,16,16]{1,2,0:T(8,128)(4,1)}, u32[]{:S(2)}) copy-start(pred[4,16,16]{1,2,0:T(8,128)(4,1)} %broadcast_compare_fusion) | copy-start | bytes 3076
  345.2 47.8 %copy-start.66 = (f32[768]{0:T(1024)S(1)}, f32[768]{0:T(1024)}, u32[]{:S(2)}) copy-start(f32[768]{0:T(1024)} %get-tuple-element.126) | copy-start | bytes 9220
  345.2 48.2 %copy-start.53 = (f32[768]{0:T(1024)S(1)}, f32[768]{0:T(1024)}, u32[]{:S(2)}) copy-start(f32[768]{0:T(1024)} %get-tuple-element.136) | copy-start | bytes 9220
  345.2 48.2 %copy-start.59 = (f32[768]{0:T(1024)S(1)}, f32[768]{0:T(1024)}, u32[]{:S(2)}) copy-start(f32[768]{0:T(1024)} %get-tuple-element.125) | copy-start | bytes 9220
  345.2 48.2 %copy-start.82 = (f32[768]{0:T(1024)S(1)}, f32[768]{0:T(1024)}, u32[]{:S(2)}) copy-start(f32[768]{0:T(1024)} %dynamic_slice.22) | copy-start | bytes 9220
  377.4 51.0 %copy-start.65 = (f32[768]{0:T(1024)S(1)}, f32[768]{0:T(1024)}, u32[]{:S(2)}) copy-start(f32[768]{0:T(1024)} %get-tuple-element.124) | copy-start | bytes 9220
  392.6 36.2 %copy-start.32 = (f32[4,16,768]{2,1,0:T(8,128)S(1)}, f32[4,16,768]{2,1,0:T(8,128)}, u32[]{:S(2)}) copy-start(f32[4,16,768]{2,1,0:T(8,128)} %copy.307) | copy-start | bytes 589828
  392.6 36.3 %copy-start.57 = (f32[768]{0:T(1024)S(1)}, f32[768]{0:T(1024)}, u32[]{:S(2)}) copy-start(f32[768]{0:T(1024)} %get-tuple-element.135) | copy-start | bytes 9220
  393.0 37.6 %copy-start.21 = (bf16[4,768,192]{2,1,0:T(8,128)(2,1)S(1)}, bf16[4,768,192]{2,1,0:T(8,128)(2,1)}, u32[]{:S(2)}) copy-start(bf16[4,768,192]{2,1,0:T(8,128)(2,1)} %dot_general.134) | copy-start | bytes 3538948
  393.1 84.1 %copy-start.19 = (f32[64,768]{1,0:T(8,128)}, f32[64,768]{1,0:T(8,128)S(1)}, u32[]{:S(2)}) copy-start(f32[64,768]{1,0:T(8,128)S(1)} %get-tuple-element.159) | copy-start | bytes 589828
  393.2 84.1 %copy-start.70 = (f32[64]{0:T(128)}, f32[64]{0:T(128)S(1)}, u32[]{:S(2)}) copy-start(f32[64]{0:T(128)S(1)} %broadcast_multiply_fusion.3) | copy-start | bytes 772
  393.4 83.9 %copy-start.71 = (f32[64]{0:T(128)}, f32[64]{0:T(128)S(1)}, u32[]{:S(2)}) copy-start(f32[64]{0:T(128)S(1)} %fusion.78) | copy-start | bytes 772
  432.1 23.1 %all-to-all-start = ((f32[4,64,768]{2,1,0:T(8,128)}), f32[4,64,768]{2,1,0:T(8,128)S(1)}, u32[]{:S(2)}, u32[]{:S(2)}) async-start(f32[4,64,768]{2,1,0:T(8,128)} %convolution_bitcast_fusion.1), calls=%async_computation | async-start | bytes 1572864 | tf_op jit(solution)/shard_map/all_to_all | solution.py:294
  435.9 350.0 %reduce-scatter.28.cloned.1.call-start = ((), (), s32[]{:S(2)}) async-start(), calls=%async_computation.17 | async-start | bytes 5529600
  455.2 44.3 %copy-start.45 = (bf16[4,16,12,64]{3,2,1,0:T(8,128)(2,1)S(1)}, bf16[4,16,12,64]{3,2,1,0:T(8,128)(2,1)}, u32[]{:S(2)}) copy-start(bf16[4,16,12,64]{3,2,1,0:T(8,128)(2,1)} %copy-done.44) | copy-start | bytes 294916
  575.9 39.1 %slice-start.7 = ((s8[6291456]{0:T(1024)(128)(4,1)}), s8[2097152]{0:T(1024)(128)(4,1)S(1)}, s32[]{:S(2)}) async-start(s8[6291456]{0:T(1024)(128)(4,1)} %bitcast.263), calls=%async_computation.29 | async-start | bytes 4194304
  732.1 91.0 %reduce-scatter.36.cloned.1.call-start = ((), (), s32[]{:S(2)}) async-start(), calls=%async_computation.21 | async-start | bytes 221184
  756.7 123.4 %reduce-scatter.26.cloned.1.call-start = ((), (), s32[]{:S(2)}) async-start(), calls=%async_computation.14 | async-start | bytes 5308416 | tf_op jit(solution)/shard_map/reduce_scatter | solution.py:351
  757.3 174.3 %reduce-scatter.20.cloned.1.call-start = ((), (), s32[]{:S(2)}) async-start(), calls=%async_computation.11 | async-start | bytes 3981312 | tf_op jit(solution)/shard_map/reduce_scatter | solution.py:351
  772.5 216.4 %reduce-scatter.22.cloned.1.call-start = ((), (), s32[]{:S(2)}) async-start(), calls=%async_computation.12 | async-start | bytes 5308416 | tf_op jit(solution)/shard_map/reduce_scatter | solution.py:351
  773.2 238.1 %reduce-scatter.32.cloned.1.call-start = ((), (), s32[]{:S(2)}) async-start(), calls=%async_computation.19 | async-start | bytes 245760
  787.7 246.8 %reduce-scatter.30.cloned.1.call-start = ((), (), s32[]{:S(2)}) async-start(), calls=%async_computation.18 | async-start | bytes 737280
  792.0 265.9 %reduce-scatter.34.cloned.1.call-start = ((), (), s32[]{:S(2)}) async-start(), calls=%async_computation.20 | async-start | bytes 737280
  806.3 182.6 %slice-start.12 = ((bf16[96,3074]{1,0:T(8,128)(2,1)}), bf16[96,2]{1,0:T(8,128)(2,1)S(1)}, s32[]{:S(2)}) async-start(bf16[96,3074]{1,0:T(8,128)(2,1)} %reduce-scatter.28.cloned.1.call-done), calls=%async_computation.34 | async-start | bytes 49152 | tf_op jit(solution)/shard_map/slice | solution.py:482
  882.3 198.3 %reduce-scatter.24.cloned.1.call-start = ((), (), s32[]{:S(2)}) async-start(), calls=%async_computation.13 | async-start | bytes 737280 | tf_op jit(solution)/shard_map/reduce_scatter | solution.py:355
  (78 other events, 633.3 us)
Sparse Core Ops, SparseCore 0:
  12.5 36.7 all-gather.16
  52.7 63.5 all-gather.18
  119.9 79.8 all-gather.20
  732.2 53.6 reduce-scatter.27
  789.4 33.6 reduce-scatter.35
  826.4 53.7 reduce-scatter.25
  883.6 47.9 reduce-scatter.19
  935.0 53.7 reduce-scatter.21
  991.7 19.5 reduce-scatter.31
  1014.0 20.4 reduce-scatter.29
  1037.3 20.5 reduce-scatter.33
  1060.0 20.4 reduce-scatter.23

commit v3 on v1

v3 whole, which is shorter than its diff:
```python
import functools

import jax
import jax.numpy as jnp
from jax import lax
from jax.experimental import pallas as pl
from jax.experimental.pallas import tpu as pltpu
from jax.sharding import PartitionSpec as P

HEADS = 12
HD = 64
SEGLEN = 128
POS = 64


NORM_EPS = 1e-05
PRECISE = lax.Precision.HIGHEST


def vector_rows(norm_gains, biases):
    return jnp.concatenate([biases, norm_gains], axis=1).T


GRANT = 60 * 1024 * 1024
INV_ROOT_TWO = 0.7071067811865476
INV_ROOT_TAU = 0.3989422804014327


def dot(left, right):
    return lax.dot_general(
        left, right, (((1,), (0,)), ((), ())), preferred_element_type=jnp.float32
    )


def dot_nt(left, right):
    return lax.dot_general(
        left, right, (((1,), (1,)), ((), ())), preferred_element_type=jnp.float32
    )


def dot_tn(left, right):
    return lax.dot_general(
        left, right, (((0,), (0,)), ((), ())), preferred_element_type=jnp.float32
    )


def norm_parts(inputs):
    average = jnp.mean(inputs, axis=-1, keepdims=True)
    centered = inputs - average
    variance = jnp.mean(centered * centered, axis=-1, keepdims=True)
    scale = lax.rsqrt(variance + NORM_EPS)
    return centered * scale, scale


def norm_pull(unit, scale, gain, upstream):
    inner = upstream * gain
    return scale * (
        inner
        - jnp.mean(inner, axis=-1, keepdims=True)
        - unit * jnp.mean(inner * unit, axis=-1, keepdims=True)
    )


def gelu_both(inputs):
    below = 0.5 * (1.0 + lax.erf(inputs * INV_ROOT_TWO))
    density = jnp.exp(-0.5 * inputs * inputs) * INV_ROOT_TAU
    return inputs * below, below + inputs * density


def row_sum(array):
    return jnp.sum(array.astype(jnp.float32), axis=0, keepdims=True)


def unfold_kernel(own_rows, packed_ref, up_ref, down_ref):
    up_wide = up_ref.shape[1]
    up_ref[...] = packed_ref[0, :, :up_wide]
    dp = packed_ref.shape[1] // own_rows
    own = down_ref.shape[1] // dp
    halves = down_ref.shape[0] // own_rows
    for place in range(dp):
        for half in range(halves):
            down_ref[
                half * own_rows : (half + 1) * own_rows, place * own : (place + 1) * own
            ] = packed_ref[
                0,
                place * own_rows : (place + 1) * own_rows,
                up_wide + half * own : up_wide + (half + 1) * own,
            ]


def unfold_feed(packed, own_rows, up_wide, down_wide):
    seg, features, both = packed.shape
    ff = seg * up_wide
    dp = features // own_rows
    own = ff // dp
    halves = down_wide // own_rows
    used = up_wide + halves * own
    if up_wide % 128 or own % 128 or own_rows % 16 or used % 128:
        down = packed[:, :, up_wide:used].reshape(seg, dp, own_rows, halves, own)
        down = down.transpose(0, 3, 2, 1, 4).reshape(features, ff)
        return unfold(packed[:, :, :up_wide]), down
    return pl.pallas_call(
        functools.partial(unfold_kernel, own_rows),
        grid=(seg,),
        in_specs=[pl.BlockSpec((1, features, used), lambda z: (z, 0, 0))],
        out_specs=[
            pl.BlockSpec((features, up_wide), lambda z: (0, z)),
            pl.BlockSpec((down_wide, ff), lambda z: (z, 0)),
        ],
        out_shape=[
            jax.ShapeDtypeStruct((features, ff), jnp.bfloat16),
            jax.ShapeDtypeStruct((features, ff), jnp.bfloat16),
        ],
        compiler_params=pltpu.CompilerParams(vmem_limit_bytes=GRANT),
        cost_estimate=pl.CostEstimate(
            flops=0, bytes_accessed=8 * features * ff, transcendentals=0
        ),
    )(packed)


def feed_kernel(
    mixed_ref, up_ref, down_ref, vec_ref, up_bias_ref, low_ref, act_ref, slope_ref, second_ref, out_ref
):
    unit, unused_scale = norm_parts(mixed_ref[...])
    first = unit * vec_ref[6:7, :] + vec_ref[4:5, :]
    low = first.astype(jnp.bfloat16)
    low_ref[...] = low
    total = first + vec_ref[3:4, :]
    ff = up_ref.shape[1]
    step = ff // 4
    for at in range(0, ff, step):
        pre = dot(low, up_ref[:, at : at + step]) + up_bias_ref[:, at : at + step]
        value, slope = gelu_both(pre)
        value = value.astype(jnp.bfloat16)
        act_ref[:, at : at + step] = value
        slope_ref[:, at : at + step] = slope.astype(jnp.bfloat16)
        total = total + dot_nt(value, down_ref[:, at : at + step])
    second_ref[...] = total
    unit, unused_scale = norm_parts(total)
    out_ref[...] = (unit * vec_ref[7:8, :] + vec_ref[5:6, :]).astype(jnp.bfloat16)


def whole_spec(shape):
    return pl.BlockSpec(shape, lambda *at: (0,) * len(shape), pipeline_mode=pl.Buffered(1))


def feed_forward(mixed, up, down, vec, up_bias):
    rows, features = mixed.shape
    ff = up.shape[1]
    tile = 256
    narrow = pl.BlockSpec((tile, features), lambda i: (i, 0))
    broad = pl.BlockSpec((tile, ff), lambda i: (i, 0))
    low = jnp.bfloat16
    return pl.pallas_call(
        feed_kernel,
        grid=(rows // tile,),
        in_specs=[
            narrow,
            whole_spec(up.shape),
            whole_spec(down.shape),
            whole_spec(vec.shape),
            whole_spec(up_bias.shape),
        ],
        out_specs=[narrow, broad, broad, narrow, narrow],
        out_shape=[
            jax.ShapeDtypeStruct((rows, features), low),
            jax.ShapeDtypeStruct((rows, ff), low),
            jax.ShapeDtypeStruct((rows, ff), low),
            jax.ShapeDtypeStruct((rows, features), jnp.float32),
            jax.ShapeDtypeStruct((rows, features), low),
        ],
        compiler_params=pltpu.CompilerParams(vmem_limit_bytes=GRANT),
        cost_estimate=pl.CostEstimate(
            flops=4 * rows * features * ff,
            bytes_accessed=4 * features * ff + 4 * rows * ff + 12 * rows * features,
            transcendentals=2 * rows * ff,
        ),
    )(mixed, up, down, vec, up_bias)


def cross_kernel(
    in_ref, grad_ref, same_ref, in_weight, out_weight, up_ref, down_ref, vec_ref, up_bias_ref,
    out_ref, source_grad_ref, context_ref, low_ref, act_ref, joined_ref, mixed_ref, pre_ref, branch_ref,
    sums_ref, up_sum_ref,
):
    features = in_ref.shape[1]
    root = HD ** (-0.5)
    inputs = in_ref[...]
    same = same_ref[...] > 0.5
    source = inputs.astype(jnp.bfloat16)
    queries = (dot(source, in_weight[:, :features]) + vec_ref[0:1, :]).astype(jnp.bfloat16)
    key_rows = dot(source, in_weight[:, features : 2 * features]).astype(jnp.bfloat16)
    values = (dot(source, in_weight[:, 2 * features :]) + vec_ref[1:2, :]).astype(jnp.bfloat16)
    two = 2 * HD
    lane = lax.broadcasted_iota(jnp.int32, (inputs.shape[0], two), 1)
    lower = lane < HD
    zero = jnp.zeros((inputs.shape[0], two), jnp.bfloat16)

    def only(half, array):
        return jnp.where(lower, array, zero) if half == 0 else jnp.where(lower, zero, array)

    weights = []
    pieces = []
    for at in range(0, features, two):
        pair = []
        for half in range(2):
            scores = dot_nt(only(half, queries[:, at : at + two]), key_rows[:, at : at + two]) * root
            scores = jnp.where(same, scores, -1e30)
            top = jnp.max(scores, axis=-1, keepdims=True)
            log_total = top + jnp.log(jnp.sum(jnp.exp(scores - top), axis=-1, keepdims=True))
            attention = jnp.exp(scores - log_total)
            weights.append(attention)
            pair.append(dot(attention.astype(jnp.bfloat16), values[:, at : at + two]))
        pieces.append(jnp.where(lower, pair[0], pair[1]).astype(jnp.bfloat16))
    context = jnp.concatenate(pieces, axis=1)
    context_ref[...] = context
    mixed = inputs + (dot(context, out_weight[...]) + vec_ref[2:3, :])
    unit_one, scale_one = norm_parts(mixed)
    first = unit_one * vec_ref[6:7, :] + vec_ref[4:5, :]
    low = first.astype(jnp.bfloat16)
    low_ref[...] = low
    ff = up_ref.shape[1]
    step = ff // 4
    slopes = []
    branch = None
    for at in range(0, ff, step):
        pre = dot(low, up_ref[:, at : at + step]) + up_bias_ref[:, at : at + step]
        value, slope = gelu_both(pre)
        slopes.append(slope)
        value = value.astype(jnp.bfloat16)
        act_ref[:, at : at + step] = value
        part = dot_nt(value, down_ref[:, at : at + step])
        branch = part if branch is None else branch + part
    unit_two, scale_two = norm_parts(first + (branch + vec_ref[3:4, :]))
    out_ref[...] = unit_two * vec_ref[7:8, :] + vec_ref[5:6, :]

    upstream = grad_ref[...]
    second_grad = norm_pull(unit_two, scale_two, vec_ref[7:8, :], upstream)
    sums_ref[5:6, :] = row_sum(upstream)
    sums_ref[7:8, :] = row_sum(upstream * unit_two)
    branch_grad = second_grad.astype(jnp.bfloat16)
    branch_ref[...] = branch_grad
    sums_ref[3:4, :] = row_sum(branch_grad)
    first_grad = second_grad
    for number, at in enumerate(range(0, ff, step)):
        part = dot(branch_grad, down_ref[:, at : at + step]) * slopes[number]
        part = part.astype(jnp.bfloat16)
        pre_ref[:, at : at + step] = part
        up_sum_ref[:, at : at + step] = row_sum(part)
        first_grad = first_grad + dot_nt(part, up_ref[:, at : at + step])
    mixed_grad = norm_pull(unit_one, scale_one, vec_ref[6:7, :], first_grad)
    sums_ref[4:5, :] = row_sum(first_grad)
    sums_ref[6:7, :] = row_sum(first_grad * unit_one)
    mixed_low = mixed_grad.astype(jnp.bfloat16)
    mixed_ref[...] = mixed_low
    sums_ref[2:3, :] = row_sum(mixed_low)
    context_grad = dot_nt(mixed_low, out_weight[...]).astype(jnp.bfloat16)
    for number, at in enumerate(range(0, features, two)):
        query_pair, key_pair, value_pair = [], [], []
        for half in range(2):
            attention = weights[2 * number + half]
            pulled = context_grad[:, at : at + two]
            value_pair.append(dot_tn(attention.astype(jnp.bfloat16), pulled))
            soft = dot_nt(only(half, pulled), values[:, at : at + two])
            score = attention * (soft - jnp.sum(soft * attention, axis=-1, keepdims=True))
            score = score.astype(jnp.bfloat16)
            query_pair.append(dot(score, key_rows[:, at : at + two]) * root)
            key_pair.append(dot_tn(score, queries[:, at : at + two]) * root)
        for base, pair in ((0, query_pair), (features, key_pair), (2 * features, value_pair)):
            joined_ref[:, base + at : base + at + two] = jnp.where(lower, pair[0], pair[1]).astype(
                jnp.bfloat16
            )
    joined = joined_ref[...]
    sums_ref[0:1, :] = row_sum(joined[:, :features])
    sums_ref[1:2, :] = row_sum(joined[:, 2 * features :])
    source_grad_ref[...] = mixed_grad + dot_nt(joined, in_weight[...])


def cross_block(inputs, upstream, same, weights, vec, up_bias):
    rows, features = inputs.shape
    ff = up_bias.shape[1]
    wide, low = jnp.float32, jnp.bfloat16
    operands = (inputs, upstream, same) + weights + (vec, up_bias)
    shapes = [
        ((rows, features), wide),
        ((rows, features), wide),
        ((rows, features), low),
        ((rows, features), low),
        ((rows, ff), low),
        ((rows, 3 * features), low),
        ((rows, features), low),
        ((rows, ff), low),
        ((rows, features), low),
        ((8, features), wide),
        ((1, ff), wide),
    ]
    return pl.pallas_call(
        cross_kernel,
        in_specs=[pl.BlockSpec(memory_space=pltpu.VMEM)] * len(operands),
        out_specs=[pl.BlockSpec(memory_space=pltpu.VMEM)] * len(shapes),
        out_shape=[jax.ShapeDtypeStruct(*shape) for shape in shapes],
        compiler_params=pltpu.CompilerParams(vmem_limit_bytes=GRANT),
        cost_estimate=pl.CostEstimate(
            flops=12 * rows * features * (2 * features + ff),
            bytes_accessed=4 * features * (2 * features + ff),
            transcendentals=3 * rows * ff,
        ),
    )(*operands)


def after(value, *earlier):
    return lax.optimization_barrier((value,) + earlier)


def total_over(array, axis_name):
    return jnp.sum(lax.all_gather(array, axis_name, axis=0, tiled=False), axis=0)


def attend_forward_kernel(token_ref, in_weight, out_weight, vec_ref, joined_ref, context_ref, total_ref, mixed_ref):
    rows, features = token_ref.shape
    root = HD ** (-0.5)
    low = jnp.bfloat16
    two = 2 * HD
    source = token_ref[...]
    joined_ref[:, :features] = (dot(source, in_weight[:, :features]) + vec_ref[0:1, :]).astype(low)
    joined_ref[:, features : 2 * features] = dot(source, in_weight[:, features : 2 * features]).astype(low)
    joined_ref[:, 2 * features :] = (dot(source, in_weight[:, 2 * features :]) + vec_ref[1:2, :]).astype(low)
    lane = lax.broadcasted_iota(jnp.int32, (SEGLEN, two), 1)
    lower = lane < HD
    zero = jnp.zeros((SEGLEN, two), low)
    for start in range(0, rows, SEGLEN):
        span = slice(start, start + SEGLEN)
        totals = jnp.zeros((SEGLEN, two), jnp.float32)
        for at in range(0, features, two):
            queries = joined_ref[span, at : at + two]
            key_rows = joined_ref[span, features + at : features + at + two]
            values = joined_ref[span, 2 * features + at : 2 * features + at + two]
            pair = []
            for half in range(2):
                kept = jnp.where(lower, queries, zero) if half == 0 else jnp.where(lower, zero, queries)
                scores = dot_nt(kept, key_rows) * root
                top = jnp.max(scores, axis=-1, keepdims=True)
                log_total = top + jnp.log(jnp.sum(jnp.exp(scores - top), axis=-1, keepdims=True))
                totals = jnp.where(lane == at // HD + half, log_total, totals)
                pair.append(dot(jnp.exp(scores - log_total).astype(low), values))
            context_ref[span, at : at + two] = jnp.where(lower, pair[0], pair[1]).astype(low)
        total_ref[span, :] = totals
    mixed_ref[...] = source.astype(jnp.float32) + (dot(context_ref[...], out_weight[...]) + vec_ref[2:3, :])


def row_blocks(tile, width):
    return pl.BlockSpec((tile, width), lambda i: (i, 0))


def attend_forward(tokens, in_weight, out_weight, vec):
    rows, features = tokens.shape
    tile = 2 * SEGLEN
    low, wide = jnp.bfloat16, jnp.float32
    outs = [(3 * features, low), (features, low), (2 * HD, wide), (features, wide)]
    return pl.pallas_call(
        attend_forward_kernel,
        grid=(rows // tile,),
        in_specs=[
            row_blocks(tile, features),
            whole_spec(in_weight.shape),
            whole_spec(out_weight.shape),
            whole_spec(vec.shape),
        ],
        out_specs=[row_blocks(tile, width) for width, unused_kind in outs],
        out_shape=[jax.ShapeDtypeStruct((rows, width), kind) for width, kind in outs],
        compiler_params=pltpu.CompilerParams(vmem_limit_bytes=GRANT),
        cost_estimate=pl.CostEstimate(
            flops=12 * rows * features * features,
            bytes_accessed=14 * rows * features + 8 * features * features,
            transcendentals=2 * rows * HEADS * SEGLEN,
        ),
    )(tokens, in_weight, out_weight, vec)


def feed_backward_kernel(
    grad_ref, second_ref, mixed_ref, slope_ref, up_ref, down_ref, vec_ref,
    branch_ref, pre_ref, mixed_grad_ref, sums_ref, up_sum_ref,
):
    @pl.when(pl.program_id(0) == 0)
    def clear():
        sums_ref[...] = jnp.zeros_like(sums_ref)
        up_sum_ref[...] = jnp.zeros_like(up_sum_ref)

    upstream = grad_ref[...].astype(jnp.float32)
    unit, scale = norm_parts(second_ref[...])
    second_grad = norm_pull(unit, scale, vec_ref[7:8, :], upstream)
    sums_ref[5:6, :] += row_sum(upstream)
    sums_ref[7:8, :] += row_sum(upstream * unit)
    branch_grad = second_grad.astype(jnp.bfloat16)
    branch_ref[...] = branch_grad
    sums_ref[3:4, :] += row_sum(branch_grad)
    first_grad = second_grad
    ff = up_ref.shape[1]
    step = ff // 4
    for at in range(0, ff, step):
        part = dot(branch_grad, down_ref[:, at : at + step]) * slope_ref[:, at : at + step].astype(jnp.float32)
        part = part.astype(jnp.bfloat16)
        pre_ref[:, at : at + step] = part
        up_sum_ref[:, at : at + step] += row_sum(part)
        first_grad = first_grad + dot_nt(part, up_ref[:, at : at + step])
    unit, scale = norm_parts(mixed_ref[...])
    mixed_grad_ref[...] = norm_pull(unit, scale, vec_ref[6:7, :], first_grad)
    sums_ref[4:5, :] += row_sum(first_grad)
    sums_ref[6:7, :] += row_sum(first_grad * unit)


def feed_backward(upstream, second, mixed, slope, up, down, vec, tile):
    rows, features = mixed.shape
    ff = up.shape[1]
    low, wide = jnp.bfloat16, jnp.float32
    narrow, broad = row_blocks(tile, features), row_blocks(tile, ff)
    return pl.pallas_call(
        feed_backward_kernel,
        grid=(rows // tile,),
        in_specs=[narrow, narrow, narrow, broad]
        + [whole_spec(array.shape) for array in (up, down, vec)],
        out_specs=[
            narrow,
            broad,
            narrow,
            pl.BlockSpec((8, features), lambda i: (0, 0)),
            pl.BlockSpec((1, ff), lambda i: (0, 0)),
        ],
        out_shape=[
            jax.ShapeDtypeStruct((rows, features), low),
            jax.ShapeDtypeStruct((rows, ff), low),
            jax.ShapeDtypeStruct((rows, features), wide),
            jax.ShapeDtypeStruct((8, features), wide),
            jax.ShapeDtypeStruct((1, ff), wide),
        ],
        compiler_params=pltpu.CompilerParams(vmem_limit_bytes=GRANT),
        cost_estimate=pl.CostEstimate(
            flops=4 * rows * features * ff,
            bytes_accessed=4 * features * ff + 4 * rows * ff + 16 * rows * features,
            transcendentals=0,
        ),
    )(upstream, second, mixed, slope, up, down, vec)


def attend_backward_kernel(
    joined_ref, total_ref, mixed_ref, patch_ref, in_weight, out_weight,
    grad_ref, low_ref, source_grad_ref, sums_ref, context_scratch,
):
    step = pl.program_id(0)

    @pl.when(step == 0)
    def clear():
        sums_ref[...] = jnp.zeros_like(sums_ref)

    rows, features = mixed_ref.shape
    root = HD ** (-0.5)
    low = jnp.bfloat16
    two = 2 * HD
    count = rows // SEGLEN
    first_row = lax.broadcasted_iota(jnp.int32, (SEGLEN, features), 0) == 0
    for number in range(count):
        span = slice(number * SEGLEN, (number + 1) * SEGLEN)
        patch = patch_ref[pl.ds(step * count + number, 1), :]
        source_grad_ref[span, :] = jnp.where(first_row, patch, mixed_ref[span, :])
    mixed_low = source_grad_ref[...].astype(low)
    low_ref[...] = mixed_low
    sums_ref[2:3, :] += row_sum(mixed_low)
    context_scratch[...] = dot_nt(mixed_low, out_weight[...]).astype(low)
    lane = lax.broadcasted_iota(jnp.int32, (SEGLEN, two), 1)
    lower = lane < HD
    zero = jnp.zeros((SEGLEN, two), low)
    for number in range(count):
        span = slice(number * SEGLEN, (number + 1) * SEGLEN)
        for at in range(0, features, two):
            queries = joined_ref[span, at : at + two]
            key_rows = joined_ref[span, features + at : features + at + two]
            values = joined_ref[span, 2 * features + at : 2 * features + at + two]
            pulled = context_scratch[span, at : at + two]
            query_pair, key_pair, value_pair = [], [], []
            for half in range(2):
                place = at // HD + half
                if half == 0:
                    kept, some = jnp.where(lower, queries, zero), jnp.where(lower, pulled, zero)
                else:
                    kept, some = jnp.where(lower, zero, queries), jnp.where(lower, zero, pulled)
                scores = dot_nt(kept, key_rows) * root
                attention = jnp.exp(scores - total_ref[span, place : place + 1])
                value_pair.append(dot_tn(attention.astype(low), pulled))
                soft = dot_nt(some, values)
                score = attention * (soft - jnp.sum(soft * attention, axis=-1, keepdims=True))
                score = score.astype(low)
                query_pair.append(dot(score, key_rows))
                key_pair.append(dot_tn(score, queries))
            grad_ref[span, at : at + two] = (jnp.where(lower, *query_pair) * root).astype(low)
            grad_ref[span, features + at : features + at + two] = (
                jnp.where(lower, *key_pair) * root
            ).astype(low)
            grad_ref[span, 2 * features + at : 2 * features + at + two] = jnp.where(
                lower, *value_pair
            ).astype(low)
    sums_ref[0:1, :] += row_sum(grad_ref[:, :features])
    sums_ref[1:2, :] += row_sum(grad_ref[:, 2 * features :])
    source_grad_ref[...] += dot_nt(grad_ref[...], in_weight[...])


def attend_backward(joined, totals, mixed_grad, patch, in_weight, out_weight):
    rows, features = mixed_grad.shape
    tile = 2 * SEGLEN
    low, wide = jnp.bfloat16, jnp.float32
    narrow, broad = row_blocks(tile, features), row_blocks(tile, 3 * features)
    return pl.pallas_call(
        attend_backward_kernel,
        grid=(rows // tile,),
        in_specs=[
            broad,
            row_blocks(tile, 2 * HD),
            narrow,
            whole_spec(patch.shape),
            whole_spec(in_weight.shape),
            whole_spec(out_weight.shape),
        ],
        out_specs=[broad, narrow, narrow, pl.BlockSpec((8, features), lambda i: (0, 0))],
        out_shape=[
            jax.ShapeDtypeStruct((rows, 3 * features), low),
            jax.ShapeDtypeStruct((rows, features), low),
            jax.ShapeDtypeStruct((rows, features), wide),
            jax.ShapeDtypeStruct((8, features), wide),
        ],
        scratch_shapes=[pltpu.VMEM((tile, features), low)],
        compiler_params=pltpu.CompilerParams(vmem_limit_bytes=GRANT),
        cost_estimate=pl.CostEstimate(
            flops=14 * rows * features * features,
            bytes_accessed=20 * rows * features + 8 * features * features,
            transcendentals=rows * HEADS * SEGLEN,
        ),
    )(joined, totals, mixed_grad, patch, in_weight, out_weight)


def pack_rows(pieces, rows):
    return jnp.concatenate([piece.reshape(rows, -1) for piece in pieces], axis=1)


def gather_local(pieces):
    joined = jnp.concatenate(pieces, axis=1)
    full = lax.all_gather(joined, ("seg", "dp"), axis=0, tiled=False)
    return full.reshape(lax.axis_size("seg"), -1, joined.shape[1])


def unfold(part):
    return part.transpose(1, 0, 2).reshape(part.shape[1], -1)


def reduce_rows(array, earlier):
    array = array.astype(jnp.bfloat16)
    if earlier is not None:
        array = after(array, earlier)[0]
    return lax.psum_scatter(array, "dp", scatter_dimension=0, tiled=True)


def reduce_columns(arrays, earlier):
    seg = lax.axis_size("seg")
    blocks = jnp.concatenate(
        [array.reshape(array.shape[0], seg, -1).transpose(1, 0, 2) for array in arrays], axis=2
    )
    blocks = after(blocks, earlier)[0]
    return lax.psum_scatter(blocks, "seg", scatter_dimension=0, tiled=True)[0].astype(jnp.float32)


def shards(
    tokens,
    cotangent,
    document_ids,
    position_ids,
    project_in,
    project_out,
    up_weight,
    down_weight,
    norm_gains,
    biases,
    up_bias,
    position_table,
):
    shard_index = lax.axis_index("seg")
    seg = lax.axis_size("seg")
    micro_count, row_count, row_tokens, features = tokens.shape
    segment_count = row_tokens // SEGLEN
    rows = micro_count * row_count
    group_count = rows * segment_count
    own_rows = project_in.shape[1]
    wide, out_wide, up_wide = project_in.shape[2], project_out.shape[2], up_weight.shape[2]
    slot_ids = jnp.arange(POS, dtype=jnp.int32)

    def mine(array):
        width = array.shape[-1] // seg
        return lax.dynamic_slice_in_dim(array, shard_index * width, width, array.ndim - 1)

    up_packed = up_bias.reshape(2, own_rows, -1).transpose(1, 0, 2).reshape(own_rows, -1)
    many = up_packed.shape[1] // 2
    small = pack_rows(
        [norm_gains.transpose(1, 0, 2), biases.transpose(1, 0, 2), up_packed, position_table],
        own_rows,
    )
    small = lax.all_gather(small, "dp", axis=0, tiled=True)
    gains_full = small[:, :4].reshape(features, 2, 2).astype(jnp.float32)
    biases_full = small[:, 4:16].reshape(features, 2, 6).astype(jnp.float32)
    up_full = small[:, 16 : 16 + 2 * many].reshape(features, 2, -1).astype(jnp.float32)
    gathered_table = small[:, 16 + 2 * many :]

    def vectors(which):
        return gains_full[:, which], biases_full[:, which], up_full[:, which].reshape(-1)

    down_wide = down_weight.shape[2]

    def turned(which):
        own = down_weight[which].T.reshape(-1, own_rows, down_weight.shape[1])
        return own.transpose(1, 0, 2).reshape(own_rows, -1)

    attend_full = gather_local([project_in[0], project_out[0]])
    feed_full = gather_local([up_weight[0], turned(0)])
    local_weights = (
        unfold(attend_full[:, :, :wide]),
        unfold(attend_full[:, :, wide:]),
        *unfold_feed(feed_full, own_rows, up_wide, down_wide),
    ) + vectors(0)
    cross_full = gather_local(
        [up_weight[1], turned(1), project_in[1], project_out[1]]
    )
    upstream = cotangent.reshape(group_count, SEGLEN, features)
    class_grad_own = upstream[:, 0, :].reshape(rows, segment_count, features)
    class_grads = lax.all_gather(class_grad_own, "seg", axis=1, tiled=True)
    flat = tokens.reshape(-1, features)
    in_weight, out_weight, up_full_local, down_full_local, gains, shifts, up_shift = local_weights
    local_vec = vector_rows(gains, shifts)
    joined, context_local, log_totals, mixed = attend_forward(flat, in_weight, out_weight, local_vec)
    first_low_local, act_local, slope, second, local_out = feed_forward(
        mixed, up_full_local, down_full_local, local_vec, up_shift[None]
    )
    local_out = local_out.reshape(upstream.shape)
    first_token = (jnp.arange(SEGLEN) == 0)[None, :, None]
    others = jnp.where(first_token, jnp.zeros((), upstream.dtype), upstream)
    branch_local, pre_local, mixed_grad, feed_sums, up_sums = feed_backward(
        others.reshape(-1, features),
        second,
        mixed,
        slope,
        up_full_local,
        down_full_local,
        local_vec,
        256,
    )
    cross_full = after(cross_full, mixed_grad)[0]
    cross_weights = (
        unfold(cross_full[:, :, 2 * up_wide : 2 * up_wide + wide]),
        unfold(cross_full[:, :, 2 * up_wide + wide :]),
        *unfold_feed(cross_full, own_rows, up_wide, down_wide),
    )
    class_own = local_out[:, 0, :].reshape(rows, segment_count, features)
    class_rows = lax.all_gather(class_own, "seg", axis=1, tiled=True)
    positions = position_ids.reshape(rows, -1)
    one_hot = (positions[:, :, None] == slot_ids).astype(jnp.bfloat16)
    cross_in = class_rows.astype(jnp.float32) + jnp.einsum(
        "rsp,dp->rsd", one_hot, gathered_table, preferred_element_type=jnp.float32
    )
    documents = document_ids.reshape(rows, -1)
    length = documents.shape[1]
    same_document = documents[:, :, None] == documents[:, None, :]
    same = jnp.where(jnp.eye(rows, dtype=bool)[:, None, :, None], same_document[:, :, None, :], False)
    gains, shifts, up_shift = vectors(1)
    (
        cross_out,
        cross_grad,
        context,
        first_low,
        activation,
        joined_grad,
        mixed_low,
        pre_gelu_grad,
        branch_grad,
        cross_sums,
        cross_up_sum,
    ) = cross_block(
        cross_in.reshape(-1, features),
        class_grads.astype(jnp.float32).reshape(-1, features),
        same.reshape(rows * length, rows * length).astype(jnp.float32),
        cross_weights,
        vector_rows(gains, shifts),
        up_shift[None],
    )
    cross_source = cross_in.astype(jnp.bfloat16).reshape(-1, features)
    cross_out = cross_out.reshape(rows, length, features)
    cross_grad = cross_grad.reshape(rows, length, features)
    cross_own = lax.dynamic_slice_in_dim(cross_out, shard_index * segment_count, segment_count, 1)
    merged = local_out.at[:, 0, :].set(
        cross_own.reshape(group_count, features).astype(jnp.bfloat16)
    )
    layer_out = merged.reshape(tokens.shape)
    cross_terms = [
        dot_tn(cross_source, mine(joined_grad)),
        dot_tn(context, mine(mixed_low)),
        dot_tn(first_low, mine(pre_gelu_grad)),
        dot_tn(activation, mine(branch_grad)),
    ]
    table_grad = jnp.einsum("rsd,rsp->dp", cross_grad, one_hot.astype(jnp.float32), precision=PRECISE)
    own_grad = lax.dynamic_slice_in_dim(cross_grad, shard_index * segment_count, segment_count, 1)
    cross_packed = pack_rows([term.astype(jnp.bfloat16) for term in cross_terms], features)
    own_grad, cross_packed = after(own_grad, cross_packed)
    cross_packed = reduce_rows(cross_packed, None)

    def class_of(array):
        return array.reshape(group_count, SEGLEN, -1)[:, 0, :]

    def with_class(array, patch):
        shape = array.shape
        array = array.reshape(group_count, SEGLEN, -1)
        return lax.dynamic_update_slice(array, patch[:, None, :], (0, 0, 0)).reshape(shape)

    class_branch, class_pre, class_mixed, class_sums, class_up_sums = feed_backward(
        own_grad.reshape(group_count, features),
        class_of(second),
        class_of(mixed),
        class_of(slope),
        up_full_local,
        down_full_local,
        local_vec,
        group_count,
    )
    feed_sums = feed_sums + class_sums
    up_sums = up_sums + class_up_sums
    down_grad = dot_tn(act_local, with_class(branch_local, class_branch)).astype(jnp.bfloat16)
    pre_local = with_class(pre_local, class_pre)
    pre_local, down_grad = after(pre_local, down_grad)
    up_grad = dot_tn(first_low_local, pre_local).astype(jnp.bfloat16)
    class_mixed, up_grad = after(class_mixed, up_grad)
    joined_local, mixed_low_local, token_grad, attend_sums = attend_backward(
        joined, log_totals, mixed_grad, class_mixed, in_weight, out_weight
    )
    outward = dot_tn(context_local, mixed_low_local).astype(jnp.bfloat16)
    inward = dot_tn(flat, joined_local).astype(jnp.bfloat16)
    input_grad = token_grad.reshape(tokens.shape)
    down_rows_sum = reduce_rows(down_grad, cross_packed)
    up_rows_sum = reduce_rows(up_grad, down_rows_sum)
    first_shard = (shard_index == 0).astype(jnp.float32)
    local_sums = jnp.concatenate([attend_sums[:3], feed_sums[3:]], axis=0)
    pieces = [
        local_sums.T,
        up_sums.reshape(features, -1),
        cross_sums.T * first_shard,
        cross_up_sum.reshape(features, -1) * first_shard,
        table_grad * first_shard,
    ]
    small_grads = reduce_rows(jnp.concatenate(pieces, axis=1), up_rows_sum)
    attend_rows = reduce_rows(jnp.concatenate([inward, outward], axis=1), small_grads)
    small_grads = total_over(small_grads.astype(jnp.float32), "seg")
    edge = 3 * features
    block_part = reduce_columns(
        [
            attend_rows[:, :edge],
            attend_rows[:, edge:],
            up_rows_sum,
            down_rows_sum.reshape(own_rows, -1, seg, down_wide)
            .transpose(0, 2, 1, 3)
            .reshape(own_rows, -1),
        ],
        attend_rows,
    )
    down_packed = down_weight.shape[1:]
    ends = [wide, wide + out_wide, wide + out_wide + up_wide]
    cross_packed = cross_packed.astype(jnp.float32)
    matrices = (
        jnp.stack([block_part[:, : ends[0]], cross_packed[:, : ends[0]]]),
        jnp.stack([block_part[:, ends[0] : ends[1]], cross_packed[:, ends[0] : ends[1]]]),
        jnp.stack([block_part[:, ends[1] : ends[2]], cross_packed[:, ends[1] : ends[2]]]),
        jnp.stack(
            [
                block_part[:, ends[2] :].reshape(down_packed),
                cross_packed[:, ends[2] :].reshape(down_packed),
            ]
        ),
    )
    start = 8 + many
    gains = jnp.stack([small_grads[:, 6:8], small_grads[:, start + 6 : start + 8]])
    bias_out = jnp.stack([small_grads[:, :6], small_grads[:, start : start + 6]])
    ups = jnp.stack(
        [small_grads[:, 8:start], small_grads[:, start + 8 : start + 8 + many]]
    ).reshape(up_bias.shape)
    return (layer_out, input_grad) + matrices + (
        gains,
        bias_out,
        ups,
        small_grads[:, start + 8 + many :],
    )


def solution(mesh):
    placed = (
        P(None, "dp", "seg", None),
        P(None, "dp", "seg", None),
        P(None, "dp", None),
        P(None, "dp", None),
        P(None, "dp", "seg"),
        P(None, "dp", "seg"),
        P(None, "dp", "seg"),
        P(None, "dp", "seg"),
        P(None, "dp", None),
        P(None, "dp", None),
        P(None, "dp"),
        P("dp", None),
    )
    return jax.shard_map(
        shards,
        mesh=mesh,
        in_specs=placed,
        out_specs=(
            P(None, "dp", "seg", None),
            P(None, "dp", "seg", None),
            P(None, "dp", "seg"),
            P(None, "dp", "seg"),
            P(None, "dp", "seg"),
            P(None, "dp", "seg"),
            P(None, "dp", None),
            P(None, "dp", None),
            P(None, "dp"),
            P("dp", None),
        ),
        check_vma=False,
    )
```

time: 973 us -> 701 us (0.72)
  Pallas kernels: 0 us -> 271 us
  matrix products: 244 us -> 52 us
  waiting for transfers between devices: 317 us -> 184 us
  other arithmetic: 125 us -> 16.2 us
  local copies, waits for them, and re-layouts: 210 us -> 104 us
    pallas_call x0 -> x8, Pallas kernels: none -> 271 us  [the longest x1 79.5 us: attend_backward(): pl.pallas_call(attend_backward_kernel, grid=(rows // tile,), in_specs=[br...]
    dot_general x36 -> x8, matrix products: 242 us -> 50.7 us  [dot_tn(): lax.dot_general(left, right, (((0,), (0,)), ((), ())), preferred_element_...]
    convert_element_type x9 -> x4, other arithmetic: 85.2 us -> 1.32 us  [the longest x1 1.14 us: reduce_columns(): lax.psum_scatter(blocks, 'seg', scatter_dimension=0, tiled=True)[0]]
    all_gather x6 -> x3, waiting for transfers between devices: 80.6 us -> 23.5 us  [gather_local(): full = lax.all_gather(joined, ('seg', 'dp'), axis=0, tiled=False)]
    unnamed x22 -> x12, waiting for transfers between devices: 132 us -> 91.5 us
    reduce_scatter x4 -> x3, waiting for transfers between devices: 105 us -> 69.5 us  [the longest x2 40.8 us: reduce_rows(): return lax.psum_scatter(array, 'dp', scatter_dimension=0, tiled=True)]
    another operation x28 -> x15, local copies, waits for them, and re-layouts: 34.2 us -> 2.37 us  [the longest x2 1.72 us: shards(): up_shift[None]]
    reshape x18 -> x10, local copies, waits for them, and re-layouts: 37.8 us -> 6.28 us  [the longest x3 3.11 us: pack_rows(): piece.reshape(rows, -1)]
  transfers between devices with their start and end apart: 16 -> 9, of which waited for: 12 -> 6; matrix products, arithmetic and copies ran while one was open for 41% -> 17% of each run, Pallas kernels for 0% -> 35%
where the time goes in v3:
time: 701 us; the launch traced here: 697 us
  Pallas kernels  271 us (39%)
  waiting for transfers between devices  184 us (26%)
  local copies, waits for them, and re-layouts  104 us (15%)
  blocking collectives  53.8 us (8%)
  matrix products  52 us (7%)
  other arithmetic  16.2 us (2%)
  between operations  14.9 us (2%)
    unnamed x12, waiting for transfers between devices  91.5 us
    pallas_call x1, Pallas kernels, attend_backward(): pl.pallas_call(attend_backward_kernel, grid=(rows // tile,), in_specs=[br...  79.5 us
    pallas_call x1, Pallas kernels, attend_forward(): pl.pallas_call(attend_forward_kernel, grid=(rows // tile,), in_specs=[row...  77.1 us
    dot_general x8, matrix products, dot_tn(): lax.dot_general(left, right, (((0,), (0,)), ((), ())), preferred_element_...  50.7 us
    pallas_call x2, Pallas kernels, feed_backward(): pl.pallas_call(feed_backward_kernel, grid=(rows // tile,), in_specs=[narr...  42.4 us
    reduce_scatter x2, waiting for transfers between devices, reduce_rows(): return lax.psum_scatter(array, 'dp', scatter_dimension=0, tiled=True)  40.8 us
    pallas_call x1, Pallas kernels, feed_forward(): pl.pallas_call(feed_kernel, grid=(rows // tile,), in_specs=[narrow, whole...  36 us
    reduce_scatter x1, waiting for transfers between devices, reduce_columns(): lax.psum_scatter(blocks, 'seg', scatter_dimension=0, tiled=True)[0]  28.6 us
  transfers between devices with their start and end apart: 9, of which 6 were waited for; matrix products, arithmetic and copies ran while one was open for 17% of the time, Pallas kernels for 35%

profile of v3, /device:TPU:0, one launch (start us, length us, event | category | flops | bytes accessed | tf_op | source)
XLA Modules:
  0.0 696.6 jit_solution(18271747521363239076)
XLA Ops:
  17.5 15.1 %all_gather.42 = bf16[4,16,768]{2,0,1:T(4,128)(2,1)S(1)} all-gather(bf16[4,4,768]{2,0,1:T(4,128)(2,1)S(1)} %copy.178), channel_id=1, replica_groups=mesh['dp'=8,'seg'=4] {'seg'}, dimensions={1}, use_global_device_ids=true | all-gather | bytes 122880 | tf_op jit(solution)/shard_map/all_gather | solution.py:630
  34.2 9.4 %all-gather.4 = bf16[8,96,88]{1,2,0:T(8,128)(2,1)S(1)} all-gather(bf16[1,96,88]{1,2,0:T(8,128)(2,1)S(1)} %maximum_bitcast_fusion.2), channel_id=1, replica_groups=mesh['dp'=8,'seg'=4] {'dp'}, dimensions={0}, use_global_device_ids=true | all-gather | bytes 152064 | tf_op jit(solution)/shard_map/all_gather | solution.py:603
  55.1 23.4 %all-gather.10.cloned.1.call-done = bf16[3072,768]{1,0:T(8,128)(2,1)} async-done(((bf16[96,768]{1,0:T(8,128)(2,1)}), bf16[3072,768]{1,0:T(8,128)(2,1)}) %all-gather.10.cloned.1.call-update) | async-done | bytes 4718608 | tf_op jit(solution)/shard_map/all_gather | solution.py:545
  78.5 4.4 slice_bitcast_fusion
  82.9 4.4 copy.165
  95.5 4.0 copy.170.in_weight
  99.5 77.1 %shard_map.195 = (bf16[2048,2304]{1,0:T(8,128)(2,1)}, bf16[2048,768]{1,0:T(8,128)(2,1)}, f32[2048,128]{1,0:T(8,128)}, f32[2048,768]{1,0:T(8,128)}) custom-call(bf16[2048,768]{1,0:T(8,128)(2,1)} %bitcast.228, bf16[768,2304]{1,0:T(8,128)(2,1)} %copy.170.in_weight, bf16[768,768]{1,0:T(8,128)(2,1)} %copy.171.out_weight, f32[8,768]{1,0:T(8,128)} %maximum_bitcast_fusion.vec_ref), custom_call_target="tpu_custom_call" | custom-call | flops 14495514624 | bytes 26738688 | tf_op jit(solution)/shard_map/pallas_call | solution.py:360
  176.6 7.8 %shard_map.196 = (bf16[768,3072]{1,0:T(8,128)(2,1)}, bf16[768,3072]{1,0:T(8,128)(2,1)}) custom-call(bf16[4,768,1536]{2,1,0:T(8,128)(2,1)} %bitcast.190), custom_call_target="tpu_custom_call" | custom-call | bytes 18874368 | tf_op jit(solution)/shard_map/pallas_call | solution.py:102
  184.4 36.0 %shard_map.197 = (bf16[2048,768]{1,0:T(8,128)(2,1)}, bf16[2048,3072]{1,0:T(8,128)(2,1)}, bf16[2048,3072]{1,0:T(8,128)(2,1)}, f32[2048,768]{1,0:T(8,128)}, bf16[2048,768]{1,0:T(8,128)(2,1)}) custom-call(f32[2048,768]{1,0:T(8,128)} %get-tuple-element.72.mixed_ref, bf16[768,3072]{1,0:T(8,128)(2,1)} %get-tuple-element.73.up_ref, ...), custom_call_target="tpu_custom_call" | custom-call | flops 19327352832 | bytes 53477376 | tf_op jit(solution)/shard_map/pallas_call | solution.py:154
  221.4 14.3 %all_gather.41 = bf16[4,16,768]{2,0,1:T(4,128)(2,1)S(1)} all-gather(bf16[4,4,768]{2,0,1:T(4,128)(2,1)S(1)} %copy.175), channel_id=1, replica_groups=mesh['dp'=8,'seg'=4] {'seg'}, dimensions={1}, use_global_device_ids=true | all-gather | bytes 122880 | tf_op jit(solution)/shard_map/all_gather | solution.py:658
  236.7 34.4 %shard_map.198 = (bf16[2048,768]{1,0:T(8,128)(2,1)}, bf16[2048,3072]{1,0:T(8,128)(2,1)}, f32[2048,768]{1,0:T(8,128)}, f32[8,768]{1,0:T(8,128)}, f32[1,3072]{1,0:T(1,128)}) custom-call(bf16[2048,768]{1,0:T(8,128)(2,1)} %bitcast_select_fusion.grad_ref, f32[2048,768]{1,0:T(8,128)} %get-tuple-element.76.second_ref, f32[2048,768]{1,0:T(8,128)} %get-tuple-element.72.mixed_ref, ...), custom_call_target="tpu_custom_call" | custom-call | flops 19327352832 | bytes 59768832 | tf_op jit(solution)/shard_map/pallas_call | solution.py:417
  273.2 4.5 slice_bitcast_fusion.1
  277.7 7.8 %shard_map.199 = (bf16[768,3072]{1,0:T(8,128)(2,1)}, bf16[768,3072]{1,0:T(8,128)(2,1)}) custom-call(bf16[4,768,2304]{2,1,0:T(8,128)(2,1)} %bitcast.187), custom_call_target="tpu_custom_call" | custom-call | bytes 18874368 | tf_op jit(solution)/shard_map/pallas_call | solution.py:102
  287.6 4.4 copy.181
  292.1 4.1 copy.184.in_weight
  296.1 20.4 %shard_map.200 = (f32[64,768]{1,0:T(8,128)}, f32[64,768]{1,0:T(8,128)}, bf16[64,768]{1,0:T(8,128)(2,1)}, bf16[64,768]{1,0:T(8,128)(2,1)}, bf16[64,3072]{1,0:T(8,...) custom-call(f32[64,768]{1,0:T(8,128)} %bitcast.200, ...), custom_call_target="tpu_custom_call" | custom-call | flops 2717908992 | bytes 14155776 | tf_op jit(solution)/shard_map/pallas_call | solution.py:297
  327.9 4.0 copy.210
  337.4 8.0 %shard_map.201 = (bf16[16,768]{1,0:T(8,128)(2,1)}, bf16[16,3072]{1,0:T(8,128)(2,1)}, f32[16,768]{1,0:T(8,128)}, f32[8,768]{1,0:T(8,128)}, f32[1,3072]{1,0:T(1,128)}) custom-call(f32[16,768]{1,0:T(8,128)} %reshape.254.grad_ref, f32[16,768]{1,0:T(8,128)} %get-tuple-element.197.second_ref, f32[16,768]{1,0:T(8,128)} %get-tuple-element.196.mixed_ref, ...), custom_call_target="tpu_custom_call" | custom-call | flops 150994944 | bytes 9830400 | tf_op jit(solution)/shard_map/pallas_call | solution.py:417
  348.4 4.4 dynamic_update_slice.6
  352.8 14.7 %convolution_convert_fusion.2 = bf16[3072,768]{1,0:T(8,128)(2,1)} fusion(bf16[2048,3072]{1,0:T(8,128)(2,1)} %get-tuple-element.98, bf16[2048,768]{1,0:T(8,128)(2,1)S(1)} %bitcast.231), kind=kOutput, calls=%fused_computation.2 | convolution fusion | flops 9666035712 | bytes 20447232 | tf_op jit(solution)/shard_map/dot_general | solution.py:42
  367.5 11.1 %reduce-scatter.19.cloned.1.call-done = bf16[96,2304]{1,0:T(8,128)(2,1)} async-done(((bf16[768,2304]{1,0:T(8,128)(2,1)}), bf16[96,2304]{1,0:T(8,128)(2,1)}) %reduce-scatter.19.cloned.1.call-update) | async-done | bytes 442384
  380.0 15.4 %convolution_convert_fusion.1 = bf16[768,3072]{1,0:T(8,128)(2,1)} fusion(bf16[2048,768]{1,0:T(8,128)(2,1)} %get-tuple-element.95, bf16[2048,3072]{1,0:T(8,128)(2,1)} %bitcast.227), kind=kOutput, calls=%fused_computation.1 | convolution fusion | flops 9666035712 | bytes 20447232 | tf_op jit(solution)/shard_map/dot_general | solution.py:42
  395.4 40.8 %reduce-scatter.13.cloned.1.call-done = bf16[384,768]{1,0:T(8,128)(2,1)} async-done(((bf16[3072,768]{1,0:T(8,128)(2,1)}), bf16[384,768]{1,0:T(8,128)(2,1)}) %reduce-scatter.13.cloned.1.call-update) | async-done | bytes 589840 | tf_op jit(solution)/shard_map/reduce_scatter | solution.py:557
  437.2 79.5 %shard_map.202 = (bf16[2048,2304]{1,0:T(8,128)(2,1)}, bf16[2048,768]{1,0:T(8,128)(2,1)}, f32[2048,768]{1,0:T(8,128)}, f32[8,768]{1,0:T(8,128)}) custom-call(bf16[2048,2304]{1,0:T(8,128)(2,1)} %get-tuple-element.83.joined_ref, f32[2048,128]{1,0:T(8,128)} %get-tuple-element.84.total_ref, f32[2048,768]{1,0:T(8,128)} %get-tuple-element.78.mixed_ref, ...), custom_call_target="tpu_custom_call" | custom-call | flops 16911433728 | bytes 36175872 | tf_op jit(solution)/shard_map/pallas_call | solution.py:511
  518.7 5.6 convolution_convert_fusion.4
  525.2 9.5 %fusion = bf16[768,2304]{0,1:T(8,128)(2,1)} fusion(bf16[2048,2304]{1,0:T(8,128)(2,1)S(1)} %copy-done.25, bf16[2048,768]{1,0:T(8,128)(2,1)S(1)} %bitcast.229), kind=kOutput, calls=%fused_computation.4 | convolution fusion | flops 7249526784 | bytes 16121856 | tf_op jit(solution)/shard_map/dot_general | solution.py:42
  535.6 4.5 pad_maximum_fusion
  540.1 29.3 %reduce-scatter.21.cloned.1.call-done = bf16[96,88]{1,0:T(8,128)(2,1)} async-done(((bf16[768,88]{1,0:T(8,128)(2,1)}), bf16[96,88]{1,0:T(8,128)(2,1)}) %reduce-scatter.21.cloned.1.call-update) | async-done | bytes 16912
  570.2 6.6 copy.214
  579.8 51.0 %reduce-scatter.23.cloned.1.call-done = bf16[96,3072]{1,0:T(8,128)(2,1)} async-done(((bf16[768,3072]{1,0:T(8,128)(2,1)}), bf16[96,3072]{1,0:T(8,128)(2,1)}) %reduce-scatter.23.cloned.1.call-update) | async-done | bytes 589840
  637.6 15.0 %all-gather.5 = f32[4,96,88]{1,2,0:T(8,128)S(1)} all-gather(f32[1,96,88]{1,2,0:T(8,128)S(1)} %bitcast_convert_fusion.2), channel_id=5, replica_groups=mesh['dp'=8,'seg'=4] {'seg'}, dimensions={0}, use_global_device_ids=true | all-gather | bytes 168960 | tf_op jit(solution)/shard_map/all_gather | solution.py:316
  655.4 28.6 %reduce-scatter.17.cloned.1.call-done = bf16[1,96,2304]{1,2,0:T(8,128)(2,1)} async-done(((bf16[4,96,2304]{1,2,0:T(8,128)(2,1)}), bf16[1,96,2304]{1,2,0:T(8,128)(2,1)}) %reduce-scatter.17.cloned.1.call-update) | async-done | bytes 442384 | tf_op jit(solution)/shard_map/reduce_scatter | solution.py:566
  (204 shorter events, 82.2 us)
Async XLA Ops:
  7.2 9.8 %copy-start.20 = (bf16[2,96,6]{1,0,2:T(2,128)(2,1)S(1)}, bf16[2,96,6]{1,0,2:T(2,128)(2,1)}, u32[]{:S(2)}) copy-start(bf16[2,96,6]{1,0,2:T(2,128)(2,1)} %param.23) | copy-start | bytes 6916
  7.2 9.9 %copy-start.1 = (bf16[2,2,512,768]{3,2,1,0:T(8,128)(2,1)S(1)}, bf16[2,2,512,768]{3,2,1,0:T(8,128)(2,1)}, u32[]{:S(2)}) copy-start(bf16[2,2,512,768]{3,2,1,0:T(8,128)(2,1)} %param.15) | copy-start | bytes 9437188
  7.2 10.0 %copy-start.21 = (bf16[2,384]{1,0:T(2,128)(2,1)S(1)}, bf16[2,384]{1,0:T(2,128)(2,1)}, u32[]{:S(2)}) copy-start(bf16[2,384]{1,0:T(2,128)(2,1)} %param.24) | copy-start | bytes 4612
  7.2 26.0 %copy-start.19 = (s32[2,2,16]{2,1,0:T(2,128)S(1)}, s32[2,2,16]{2,1,0:T(2,128)}, u32[]{:S(2)}) copy-start(s32[2,2,16]{2,1,0:T(2,128)} %param.16) | copy-start | bytes 772
  7.2 26.9 %copy-start.14 = (bf16[96,64]{0,1:T(8,128)(2,1)S(1)}, bf16[96,64]{0,1:T(8,128)(2,1)}, u32[]{:S(2)}) copy-start(bf16[96,64]{0,1:T(8,128)(2,1)} %param.25) | copy-start | bytes 36868
  7.2 26.9 %copy-start.22 = (bf16[2,96,2]{1,2,0:T(2,128)(2,1)S(1)}, bf16[2,96,2]{1,2,0:T(2,128)(2,1)}, u32[]{:S(2)}) copy-start(bf16[2,96,2]{1,2,0:T(2,128)(2,1)} %param.22) | copy-start | bytes 2308
  7.2 71.3 %all-gather.10.cloned.1.call-start = ((), (), s32[]{:S(2)}) async-start(), calls=%async_computation.9 | async-start | bytes 4866048 | tf_op jit(solution)/shard_map/all_gather | solution.py:545
  10.7 165.9 %all-gather.12.cloned.1.call-start = ((), (), s32[]{:S(2)}) async-start(), calls=%async_computation.10 | async-start | bytes 9732096 | tf_op jit(solution)/shard_map/all_gather | solution.py:545
  14.2 256.9 %all-gather.14.cloned.1.call-start = ((), (), s32[]{:S(2)}) async-start(), calls=%async_computation.11 | async-start | bytes 14598144 | tf_op jit(solution)/shard_map/all_gather | solution.py:545
  17.0 361.6 %reduce-scatter.19.cloned.1.call-start = ((), (), s32[]{:S(2)}) async-start(), calls=%async_computation.12 | async-start | bytes 3981312
  184.3 51.4 %copy-start.5 = (bf16[768,88]{0,1:T(8,128)(2,1)S(1)}, bf16[768,88]{0,1:T(8,128)(2,1)}, u32[]{:S(2)}) copy-start(bf16[768,88]{0,1:T(8,128)(2,1)} %copy-done.4) | copy-start | bytes 405508
  184.3 51.4 %copy-start.18 = (s32[2,2,16]{2,1,0:T(2,128)S(1)}, s32[2,2,16]{2,1,0:T(2,128)}, u32[]{:S(2)}) copy-start(s32[2,2,16]{2,1,0:T(2,128)} %param.17) | copy-start | bytes 772
  318.1 5.4 copy-start.10
  318.1 6.6 copy-start.6
  318.8 7.3 %copy-start.9 = (bf16[64,768]{1,0:T(8,128)(2,1)S(1)}, bf16[64,768]{1,0:T(8,128)(2,1)}, u32[]{:S(2)}) copy-start(bf16[64,768]{1,0:T(8,128)(2,1)} %get-tuple-element.89) | copy-start | bytes 294916
  321.9 5.6 copy-start
  331.9 4.9 copy-start.8
  331.9 104.3 %reduce-scatter.13.cloned.1.call-start = ((), (), s32[]{:S(2)}) async-start(), calls=%async_computation.6 | async-start | bytes 5308416 | tf_op jit(solution)/shard_map/reduce_scatter | solution.py:557
  337.4 9.8 %copy-start.24 = (bf16[2048,768]{1,0:T(8,128)(2,1)S(1)}, bf16[2048,768]{1,0:T(8,128)(2,1)}, u32[]{:S(2)}) copy-start(bf16[2048,768]{1,0:T(8,128)(2,1)} %get-tuple-element.99) | copy-start | bytes 9437188
  380.0 154.8 %reduce-scatter.15.cloned.1.call-start = ((), (), s32[]{:S(2)}) async-start(), calls=%async_computation.7 | async-start | bytes 5308416 | tf_op jit(solution)/shard_map/reduce_scatter | solution.py:557
  395.4 41.1 %copy-start.15 = (f32[1,3072]{1,0:T(1,128)S(1)}, f32[1,3072]{1,0:T(1,128)}, u32[]{:S(2)}) copy-start(f32[1,3072]{1,0:T(1,128)} %get-tuple-element.113) | copy-start | bytes 36868
  436.3 133.1 %reduce-scatter.21.cloned.1.call-start = ((), (), s32[]{:S(2)}) async-start(), calls=%async_computation.13 | async-start | bytes 221184
  437.1 80.4 %copy-start.16 = (f32[1,3072]{1,0:T(1,128)S(1)}, f32[1,3072]{1,0:T(1,128)}, u32[]{:S(2)}) copy-start(f32[1,3072]{1,0:T(1,128)} %get-tuple-element.110) | copy-start | bytes 36868
  437.2 80.3 %copy-start.17 = (f32[1,3072]{1,0:T(1,128)S(1)}, f32[1,3072]{1,0:T(1,128)}, u32[]{:S(2)}) copy-start(f32[1,3072]{1,0:T(1,128)} %get-tuple-element.111) | copy-start | bytes 36868
  437.2 80.9 %copy-start.12 = (f32[8,768]{1,0:T(8,128)S(1)}, f32[8,768]{1,0:T(8,128)}, u32[]{:S(2)}) copy-start(f32[8,768]{1,0:T(8,128)} %get-tuple-element.108) | copy-start | bytes 73732
  437.2 80.9 %copy-start.13 = (f32[8,768]{1,0:T(8,128)S(1)}, f32[8,768]{1,0:T(8,128)}, u32[]{:S(2)}) copy-start(f32[8,768]{1,0:T(8,128)} %get-tuple-element.109) | copy-start | bytes 73732
  437.2 81.0 %copy-start.11 = (f32[8,768]{1,0:T(8,128)S(1)}, f32[8,768]{1,0:T(8,128)}, u32[]{:S(2)}) copy-start(f32[8,768]{1,0:T(8,128)} %get-tuple-element.112) | copy-start | bytes 73732
  437.2 81.0 %copy-start.7 = (f32[64,768]{1,0:T(8,128)S(1)}, f32[64,768]{1,0:T(8,128)}, u32[]{:S(2)}) copy-start(f32[64,768]{1,0:T(8,128)} %get-tuple-element.85) | copy-start | bytes 589828
  518.7 5.7 copy-start.23
  518.7 6.5 copy-start.25
  535.5 95.2 %reduce-scatter.23.cloned.1.call-start = ((), (), s32[]{:S(2)}) async-start(), calls=%async_computation.14 | async-start | bytes 5308416
  576.8 107.2 %reduce-scatter.17.cloned.1.call-start = ((), (), s32[]{:S(2)}) async-start(), calls=%async_computation.8 | async-start | bytes 2949120 | tf_op jit(solution)/shard_map/reduce_scatter | solution.py:566
  (3 other events, 5.6 us)
Sparse Core Ops, SparseCore 0:
  11.5 66.9 all-gather.9
  82.0 80.4 all-gather.11
  165.9 101.4 all-gather.13
  332.0 46.5 reduce-scatter.18
  382.5 53.7 reduce-scatter.12
  439.5 53.7 reduce-scatter.14
  535.7 33.6 reduce-scatter.20
  577.0 53.7 reduce-scatter.22
  634.3 49.7 reduce-scatter.16
